TPU v7x, 32 devices: a whole 2x2x4 slice. The times are simulated.
32 devices in a mesh: seq: 16 (over z, y, x), head: 2 (over core).
Axes of the slice: x: 2, y: 2, z: 4, core: 2. Of those that a mesh axis runs over, the one named last changes fastest.
Arguments:
- tokens: bfloat16 [10240, 768], P('seq', 'head'), may hold values from -6 to 6
- image_starts: int32 [54], replicated, may hold values from 0 to 10240, as said below
- ln_gain: float32 [768], replicated, may hold values from 0.1 to 1.9
- w_qkv: bfloat16 [768, 3, 768], P(None, None, 'head'), may hold values from -0.21875 to 0.21875
- q_gain: float32 [64], replicated, may hold values from 0.8 to 2
- k_gain: float32 [64], replicated, may hold values from 0.8 to 2
- w_up: bfloat16 [768, 3072], P(None, 'head'), may hold values from -0.21875 to 0.21875
- up_bias: float32 [3072], P('head'), may hold values from -3 to 3
- w_attn_out: bfloat16 [768, 768], P('head'), may hold values from -1.25 to 1.25
- w_down: bfloat16 [3072, 768], P('head'), may hold values from -0.109375 to 0.109375
- out_bias: float32 [768], P('head'), may hold values from -3 to 3
- cotangent: bfloat16 [10240, 768], P('seq', 'head'), may hold values from -8 to 8
Outputs:
- block_out: bfloat16 [10240, 768], P('seq', 'head')
- tokens_grad: bfloat16 [10240, 768], P('seq', 'head')
- ln_gain_grad: float32 [768], P('head')
- w_qkv_grad: float32 [768, 3, 768], P(None, None, 'head')
- q_gain_grad: float32 [64], P('head')
- k_gain_grad: float32 [64], P('head')
- w_up_grad: float32 [768, 3072], P(None, 'head')
- up_bias_grad: float32 [3072], P('head')
- w_attn_out_grad: float32 [768, 768], P('head')
- w_down_grad: float32 [3072, 768], P('head')
- out_bias_grad: float32 [768], P('head')
Inputs may be any that keep to these rules, and one draw needn't show every extreme that they name: image_starts[0] is 0 and the entries rise strictly until they reach 10240; all later entries equal 10240 and are unused. Image i holds the tokens from its start up to the next entry minus one; every image holds 196 or 3136 tokens except the last, which may be cut short, and at least one holds exactly 3136.
All inputs are finite; a program needn't handle non-finite values.
Results may differ from a plain program's by a relative error of at most 0.012.
Values may be sent and summed in bfloat16 or wider, within the bound.
No kernel may reach another device: no remote copies, remote signals or barrier semaphores. Data moves between devices by JAX's collectives and lax.ppermute only.
A program may use at most 192 MiB of HBM per device.

v0:
```python
import jax
import jax.numpy as jnp
from jax import lax
from jax.sharding import PartitionSpec as P

HS = 64
LONG_LEN = 3136


EPSILON = 1e-06
MASKED = -1e30


def from_behind(block, axis, distance):
    devices = range(lax.axis_size(axis))
    route = [(i - distance, i) for i in devices if i - distance in devices]
    return lax.ppermute(block, axis, route)


def layer_norm(values, gain_row):
    row_mean = jnp.mean(values, axis=-1, keepdims=True)
    centred = values - row_mean
    spread = jnp.mean(centred * centred, axis=-1, keepdims=True)
    return centred * lax.rsqrt(spread + EPSILON) * gain_row


def exact_gelu(values):
    return jax.nn.gelu(values, approximate=False)


def image_ids(image_starts, positions):
    return jnp.sum((image_starts[None, :] <= positions[:, None]).astype(jnp.int32), axis=1)


def head_scores(queries, key_part, query_images, key_images):
    scores = jnp.einsum("qhc,khc->hqk", queries, key_part, preferred_element_type=jnp.float32)
    same_image = query_images[:, None] == key_images[None, :]
    return jnp.where(same_image[None], scores, MASKED)


def on_device(
    tokens,
    image_starts,
    ln_gain,
    w_qkv,
    q_gain,
    k_gain,
    w_up,
    up_bias,
    w_attn_out,
    w_down,
    out_bias,
    cotangent,
):
    tok_rows = tokens.shape[0]
    local_width = w_qkv.shape[2]
    local_heads = local_width // HS
    shaped = (tok_rows, local_heads, HS)
    reach_dev = (LONG_LEN + tok_rows - 2) // tok_rows
    cycle_size = lax.axis_size("seq")
    cycle_place = lax.axis_index("seq")
    row_index = jnp.arange(tok_rows, dtype=jnp.int32)
    query_images = image_ids(image_starts, cycle_place * tok_rows + row_index)
    q_scale = HS ** (-0.5)
    gathered = lax.all_gather(tokens, "head", axis=1, tiled=True)
    normed_f, norm_pull = jax.vjp(layer_norm, gathered.astype(jnp.float32), ln_gain)
    normed = normed_f.astype(jnp.bfloat16)
    projected = jnp.einsum("td,dkc->tkc", normed, w_qkv, preferred_element_type=jnp.float32)

    def query_norm(raw_heads, gain_row):
        return layer_norm(raw_heads, gain_row) * q_scale

    query_f, query_pull = jax.vjp(query_norm, projected[:, 0].reshape(shaped), q_gain)
    key_f, key_pull = jax.vjp(layer_norm, projected[:, 1].reshape(shaped), k_gain)
    queries = query_f.astype(jnp.bfloat16)
    key_heads = key_f.astype(jnp.bfloat16)
    values = projected[:, 2].astype(jnp.bfloat16)
    up_input = jnp.dot(normed, w_up, preferred_element_type=jnp.float32) + up_bias
    hidden_f, gelu_pull = jax.vjp(exact_gelu, up_input)
    hidden = hidden_f.astype(jnp.bfloat16)
    own_block = jnp.stack([key_heads.reshape(tok_rows, local_width), values])

    def pass_up(carried, unused):
        arrived = from_behind(carried, "seq", 1)
        return (arrived, arrived)

    def pass_down(carried, unused):
        arrived = from_behind(carried, "seq", -1)
        return (arrived, arrived)

    from_below = lax.scan(pass_up, own_block, None, length=reach_dev)[1]
    from_above = lax.scan(pass_down, own_block, None, length=reach_dev)[1]
    blocks = jnp.concatenate([own_block[None], from_below, from_above], axis=0)
    offsets = jnp.array(
        [0] + list(range(1, reach_dev + 1)) + [-distance for distance in range(1, reach_dev + 1)],
        dtype=jnp.int32,
    )
    sources = jnp.mod(cycle_place - offsets, cycle_size)

    def sweep(update, initial):

        def advance(carried, inputs):
            kv_block, source = inputs
            key_images = image_ids(image_starts, source * tok_rows + row_index)
            return update(carried, kv_block, key_images)

        return lax.scan(advance, initial, (blocks, sources))

    empty_mark = jnp.zeros((), jnp.float32)

    def online_update(carried, kv_block, key_images):
        row_peak, row_total, running = carried
        scores = head_scores(queries, kv_block[0].reshape(shaped), query_images, key_images)
        new_peak = jnp.maximum(row_peak, jnp.max(scores, axis=-1))
        rescale = jnp.exp(row_peak - new_peak)
        probs = jnp.exp(scores - new_peak[..., None])
        row_total = row_total * rescale + jnp.sum(probs, axis=-1)
        added = jnp.einsum(
            "hqk,khc->qhc",
            probs.astype(jnp.bfloat16),
            kv_block[1].reshape(shaped),
            preferred_element_type=jnp.float32,
        )
        running = running * jnp.transpose(rescale)[..., None] + added
        return ((new_peak, row_total, running), empty_mark)

    start_peak = jnp.full((local_heads, tok_rows), MASKED, jnp.float32)
    start_total = jnp.zeros((local_heads, tok_rows), jnp.float32)
    start_mix = jnp.zeros(shaped, jnp.float32)
    (row_peak, row_total, running), unused_marks = sweep(
        online_update, (start_peak, start_total, start_mix)
    )
    log_total = row_peak + jnp.log(row_total)
    mixture = running / jnp.transpose(row_total)[..., None]
    attended = mixture.reshape(tok_rows, local_width).astype(jnp.bfloat16)
    partial_out = jnp.dot(attended, w_attn_out, preferred_element_type=jnp.float32) + jnp.dot(
        hidden, w_down, preferred_element_type=jnp.float32
    )
    summed = lax.psum_scatter(
        partial_out.astype(jnp.bfloat16), "head", scatter_dimension=1, tiled=True
    ).astype(jnp.float32)
    block_out = (summed + tokens.astype(jnp.float32) + out_bias).astype(jnp.bfloat16)
    cot_whole = lax.all_gather(cotangent, "head", axis=1, tiled=True)
    d_attended = jnp.einsum(
        "td,cd->tc", cot_whole, w_attn_out, preferred_element_type=jnp.float32
    ).astype(jnp.bfloat16)
    d_hidden = jnp.einsum("td,fd->tf", cot_whole, w_down, preferred_element_type=jnp.float32)
    d_upper = gelu_pull(d_hidden)[0].astype(jnp.bfloat16)
    grad_attn_out = jnp.einsum("tc,td->cd", attended, cot_whole, preferred_element_type=jnp.float32)
    grad_down = jnp.einsum("tf,td->fd", hidden, cot_whole, preferred_element_type=jnp.float32)
    grad_out_bias = jnp.sum(cotangent.astype(jnp.float32), axis=0)
    grad_up_bias = jnp.sum(d_upper.astype(jnp.float32), axis=0)
    grad_up = jnp.einsum("td,tf->df", normed, d_upper, preferred_element_type=jnp.float32)
    d_normed = jnp.einsum("tf,df->td", d_upper, w_up, preferred_element_type=jnp.float32)
    d_heads = d_attended.reshape(shaped)
    delta_rows = jnp.einsum("qhc,qhc->hq", d_heads.astype(jnp.float32), mixture)

    def grad_update(carried, kv_block, key_images):
        key_part = kv_block[0].reshape(shaped)
        value_part = kv_block[1].reshape(shaped)
        scores = head_scores(queries, key_part, query_images, key_images)
        weights = jnp.exp(scores - log_total[..., None])
        d_weights = jnp.einsum(
            "qhc,khc->hqk", d_heads, value_part, preferred_element_type=jnp.float32
        )
        d_scores = (weights * (d_weights - delta_rows[..., None])).astype(jnp.bfloat16)
        d_query = carried + jnp.einsum(
            "hqk,khc->qhc", d_scores, key_part, preferred_element_type=jnp.float32
        )
        d_key = jnp.einsum("hqk,qhc->khc", d_scores, queries, preferred_element_type=jnp.float32)
        d_value = jnp.einsum(
            "hqk,qhc->khc",
            weights.astype(jnp.bfloat16),
            d_heads,
            preferred_element_type=jnp.float32,
        )
        return (
            d_query,
            jnp.stack(
                [d_key.reshape(tok_rows, local_width), d_value.reshape(tok_rows, local_width)]
            ),
        )

    empty_grad = jnp.zeros((2, tok_rows, local_width), jnp.float32)
    d_queries, returned = sweep(grad_update, jnp.zeros(shaped, jnp.float32))
    own_part = returned[0]
    to_below = returned[1 : reach_dev + 1]
    to_above = returned[reach_dev + 1 :]

    def back_down(carried, addend):
        return (
            from_behind((carried + addend).astype(jnp.bfloat16), "seq", -1).astype(jnp.float32),
            None,
        )

    def back_up(carried, addend):
        return (
            from_behind((carried + addend).astype(jnp.bfloat16), "seq", 1).astype(jnp.float32),
            None,
        )

    home_below = lax.scan(back_down, empty_grad, to_below[::-1])[0]
    home_above = lax.scan(back_up, empty_grad, to_above[::-1])[0]
    kv_grad = own_part + home_below + home_above
    d_query_raw, d_q_gain = query_pull(d_queries)
    d_key_raw, d_k_gain = key_pull(kv_grad[0].reshape(shaped))
    d_proj = jnp.stack(
        [
            d_query_raw.reshape(tok_rows, local_width),
            d_key_raw.reshape(tok_rows, local_width),
            kv_grad[1],
        ],
        axis=1,
    ).astype(jnp.bfloat16)
    grad_qkv = jnp.einsum("td,tkc->dkc", normed, d_proj, preferred_element_type=jnp.float32)
    d_normed = d_normed + jnp.einsum(
        "tkc,dkc->td", d_proj, w_qkv, preferred_element_type=jnp.float32
    )
    d_input, d_ln = norm_pull(d_normed)
    gain_parts = jnp.stack([d_q_gain, d_k_gain])
    input_sum, ln_share, gain_share = (
        lax.psum_scatter(
            d_input.astype(jnp.bfloat16), "head", scatter_dimension=1, tiled=True
        ).astype(jnp.float32),
        lax.psum_scatter(
            d_ln[None, :].astype(jnp.bfloat16), "head", scatter_dimension=1, tiled=True
        ).astype(jnp.float32),
        lax.psum_scatter(
            gain_parts.astype(jnp.bfloat16), "head", scatter_dimension=1, tiled=True
        ).astype(jnp.float32),
    )
    tokens_grad = (input_sum + cotangent.astype(jnp.float32)).astype(jnp.bfloat16)
    totals = lax.psum(
        (
            grad_qkv,
            grad_up,
            grad_attn_out,
            grad_down,
            grad_up_bias,
            grad_out_bias,
            ln_share[0],
            gain_share,
        ),
        "seq",
    )
    return (
        block_out,
        tokens_grad,
        totals[6],
        totals[0],
        totals[7][0],
        totals[7][1],
        totals[1],
        totals[4],
        totals[2],
        totals[3],
        totals[5],
    )


def solution(mesh):
    in_specs = (
        P("seq", "head"),
        P(),
        P(),
        P(None, None, "head"),
        P(),
        P(),
        P(None, "head"),
        P("head"),
        P("head", None),
        P("head", None),
        P("head"),
        P("seq", "head"),
    )
    out_specs = (
        P("seq", "head"),
        P("seq", "head"),
        P("head"),
        P(None, None, "head"),
        P("head"),
        P("head"),
        P(None, "head"),
        P("head"),
        P("head", None),
        P("head", None),
        P("head"),
    )
    return jax.shard_map(
        on_device, mesh=mesh, in_specs=in_specs, out_specs=out_specs, check_vma=False
    )
```

profile of v0, /device:TPU:0, one launch (start us, length us, event | category | flops | bytes accessed | tf_op | source)
XLA Modules:
  0.0 1638.3 jit_solution(14547607958051637688)
XLA Ops:
  36.0 157.1 %while.74 = (s32[]{:T(128)}, bf16[2,640,384]{2,1,0:T(8,128)(2,1)}, bf16[5,2,640,384]{2,3,1,0:T(8,128)(2,1)}, s32[]{:T(128)}) while((s32[]{:T(128)}, bf16[2,640,384]{2,1,0:T(8,128)(2,1)}, bf16[5,2,640,384]{2,3,1,0:T(8,128)(2,1)}, s32[]{:T(128)}) %tuple.135), condition=%wide.region_5.0_spmd, body=%wide.region_4.0_spmd.sunk | while | flops 2 | bytes 9830505 | solution.py:91
  41.7 20.7 %collective-permute-done = bf16[2,640,384]{2,1,0:T(8,128)(2,1)} collective-permute-done((bf16[2,640,384]{2,1,0:T(8,128)(2,1)}, bf16[2,640,384]{2,1,0:T(8,128)(2,1)}, u32[]{:S(2)}, u32[]{:S(2)}) %collective-permute-start) | collective-permute-done | bytes 983072 | tf_op jit(solution)/shard_map/while/body/eval_jaxpr/ppermute | solution.py:17
  74.4 19.8 %collective-permute-done = bf16[2,640,384]{2,1,0:T(8,128)(2,1)} collective-permute-done((bf16[2,640,384]{2,1,0:T(8,128)(2,1)}, bf16[2,640,384]{2,1,0:T(8,128)(2,1)}, u32[]{:S(2)}, u32[]{:S(2)}) %collective-permute-start) | collective-permute-done | bytes 983072 | tf_op jit(solution)/shard_map/while/body/eval_jaxpr/ppermute | solution.py:17
  106.2 19.0 %collective-permute-done = bf16[2,640,384]{2,1,0:T(8,128)(2,1)} collective-permute-done((bf16[2,640,384]{2,1,0:T(8,128)(2,1)}, bf16[2,640,384]{2,1,0:T(8,128)(2,1)}, u32[]{:S(2)}, u32[]{:S(2)}) %collective-permute-start) | collective-permute-done | bytes 983072 | tf_op jit(solution)/shard_map/while/body/eval_jaxpr/ppermute | solution.py:17
  138.1 18.1 %collective-permute-done = bf16[2,640,384]{2,1,0:T(8,128)(2,1)} collective-permute-done((bf16[2,640,384]{2,1,0:T(8,128)(2,1)}, bf16[2,640,384]{2,1,0:T(8,128)(2,1)}, u32[]{:S(2)}, u32[]{:S(2)}) %collective-permute-start) | collective-permute-done | bytes 983072 | tf_op jit(solution)/shard_map/while/body/eval_jaxpr/ppermute | solution.py:17
  169.1 17.2 %collective-permute-done = bf16[2,640,384]{2,1,0:T(8,128)(2,1)} collective-permute-done((bf16[2,640,384]{2,1,0:T(8,128)(2,1)}, bf16[2,640,384]{2,1,0:T(8,128)(2,1)}, u32[]{:S(2)}, u32[]{:S(2)}) %collective-permute-start) | collective-permute-done | bytes 983072 | tf_op jit(solution)/shard_map/while/body/eval_jaxpr/ppermute | solution.py:17
  195.9 144.9 %while.75 = (s32[]{:T(128)}, bf16[2,640,384]{2,1,0:T(8,128)(2,1)}, bf16[5,2,640,384]{2,3,1,0:T(8,128)(2,1)}, s32[]{:T(128)}) while((s32[]{:T(128)}, bf16[2,640,384]{2,1,0:T(8,128)(2,1)}, bf16[5,2,640,384]{2,3,1,0:T(8,128)(2,1)}, s32[]{:T(128)}) %tuple.132), condition=%wide.region_7.8_spmd, body=%wide.region_6.0_spmd.sunk | while | flops 2 | bytes 9830505 | solution.py:92
  197.1 22.1 %collective-permute-done.1 = bf16[2,640,384]{2,1,0:T(8,128)(2,1)} collective-permute-done((bf16[2,640,384]{2,1,0:T(8,128)(2,1)}, bf16[2,640,384]{2,1,0:T(8,128)(2,1)}, u32[]{:S(2)}, u32[]{:S(2)}) %collective-permute-start.1) | collective-permute-done | bytes 983072 | tf_op jit(solution)/shard_map/while/body/eval_jaxpr/ppermute | solution.py:17
  227.2 21.5 %collective-permute-done.1 = bf16[2,640,384]{2,1,0:T(8,128)(2,1)} collective-permute-done((bf16[2,640,384]{2,1,0:T(8,128)(2,1)}, bf16[2,640,384]{2,1,0:T(8,128)(2,1)}, u32[]{:S(2)}, u32[]{:S(2)}) %collective-permute-start.1) | collective-permute-done | bytes 983072 | tf_op jit(solution)/shard_map/while/body/eval_jaxpr/ppermute | solution.py:17
  256.8 20.8 %collective-permute-done.1 = bf16[2,640,384]{2,1,0:T(8,128)(2,1)} collective-permute-done((bf16[2,640,384]{2,1,0:T(8,128)(2,1)}, bf16[2,640,384]{2,1,0:T(8,128)(2,1)}, u32[]{:S(2)}, u32[]{:S(2)}) %collective-permute-start.1) | collective-permute-done | bytes 983072 | tf_op jit(solution)/shard_map/while/body/eval_jaxpr/ppermute | solution.py:17
  285.6 21.2 %collective-permute-done.1 = bf16[2,640,384]{2,1,0:T(8,128)(2,1)} collective-permute-done((bf16[2,640,384]{2,1,0:T(8,128)(2,1)}, bf16[2,640,384]{2,1,0:T(8,128)(2,1)}, u32[]{:S(2)}, u32[]{:S(2)}) %collective-permute-start.1) | collective-permute-done | bytes 983072 | tf_op jit(solution)/shard_map/while/body/eval_jaxpr/ppermute | solution.py:17
  314.9 19.1 %collective-permute-done.1 = bf16[2,640,384]{2,1,0:T(8,128)(2,1)} collective-permute-done((bf16[2,640,384]{2,1,0:T(8,128)(2,1)}, bf16[2,640,384]{2,1,0:T(8,128)(2,1)}, u32[]{:S(2)}, u32[]{:S(2)}) %collective-permute-start.1) | collective-permute-done | bytes 983072 | tf_op jit(solution)/shard_map/while/body/eval_jaxpr/ppermute | solution.py:17
  350.8 203.0 %while.76 = (s32[]{:T(128)}, f32[6,640]{1,0:T(8,128)S(1)}, f32[6,640]{1,0:T(8,128)S(1)}, f32[640,6,64]{0,2,1:T(8,128)}, s32[640]{0:T(1024)S(1)}, /*index=5*/s32[...) while((s32[]{:T(128)}, f32[6,640]{1,0:T(8,128)S(1)}, ...), condition=%wide.region_15.16_spmd.clone, body=%wide.region_11.15_spmd.clone.sunk | while | flops 650080000 | bytes 76116904 | solution.py:107
  560.9 243.3 %while.77 = (s32[]{:T(128)}, f32[640,6,64]{0,2,1:T(8,128)}, f32[11,2,640,384]{2,3,1,0:T(8,128)}, bf16[11,2,640,384]{2,3,1,0:T(8,128)(2,1)}, s32[640]{0:T(1024)S(...) while((s32[]{:T(128)}, f32[640,6,64]{0,2,1:T(8,128)}, ...), condition=%wide.region_19.20_spmd.clone, body=%wide.region_17.19_spmd.clone.sunk | while | flops 1594021120 | bytes 78457272 | solution.py:107
  807.9 23.3 %copy.65 = f32[11,2,640,384]{3,2,1,0:T(8,128)} copy(f32[11,2,640,384]{2,3,1,0:T(8,128)} %get-tuple-element.202) | data formatting | bytes 43253760 | tf_op jit(solution)/shard_map/while | solution.py:107
  854.5 153.6 %while.78 = (s32[]{:T(128)}, f32[2,640,384]{2,1,0:T(8,128)}, f32[5,2,640,384]{3,2,1,0:T(8,128)}, s32[]{:T(128)}, s32[]{:T(128)}) while((s32[]{:T(128)}, f32[2,640,384]{2,1,0:T(8,128)}, f32[5,2,640,384]{3,2,1,0:T(8,128)}, s32[]{:T(128)}, s32[]{:T(128)}) %tuple.147), condition=%wide.region_23.24_spmd.clone, body=%wide.region_22.23_spmd.clone.sunk | while | flops 1966083 | bytes 11796595 | solution.py:202
  857.5 25.7 %collective-permute-done.2 = bf16[2,640,384]{2,1,0:T(8,128)(2,1)} collective-permute-done((bf16[2,640,384]{2,1,0:T(8,128)(2,1)S(1)}, bf16[2,640,384]{2,1,0:T(8,128)(2,1)}, u32[]{:S(2)}, u32[]{:S(2)}) %collective-permute-start.2) | collective-permute-done | bytes 983072 | tf_op jit(solution)/shard_map/while/body/eval_jaxpr/ppermute | solution.py:17
  889.6 25.4 %collective-permute-done.2 = bf16[2,640,384]{2,1,0:T(8,128)(2,1)} collective-permute-done((bf16[2,640,384]{2,1,0:T(8,128)(2,1)S(1)}, bf16[2,640,384]{2,1,0:T(8,128)(2,1)}, u32[]{:S(2)}, u32[]{:S(2)}) %collective-permute-start.2) | collective-permute-done | bytes 983072 | tf_op jit(solution)/shard_map/while/body/eval_jaxpr/ppermute | solution.py:17
  921.2 25.1 %collective-permute-done.2 = bf16[2,640,384]{2,1,0:T(8,128)(2,1)} collective-permute-done((bf16[2,640,384]{2,1,0:T(8,128)(2,1)S(1)}, bf16[2,640,384]{2,1,0:T(8,128)(2,1)}, u32[]{:S(2)}, u32[]{:S(2)}) %collective-permute-start.2) | collective-permute-done | bytes 983072 | tf_op jit(solution)/shard_map/while/body/eval_jaxpr/ppermute | solution.py:17
  952.7 23.7 %collective-permute-done.2 = bf16[2,640,384]{2,1,0:T(8,128)(2,1)} collective-permute-done((bf16[2,640,384]{2,1,0:T(8,128)(2,1)S(1)}, bf16[2,640,384]{2,1,0:T(8,128)(2,1)}, u32[]{:S(2)}, u32[]{:S(2)}) %collective-permute-start.2) | collective-permute-done | bytes 983072 | tf_op jit(solution)/shard_map/while/body/eval_jaxpr/ppermute | solution.py:17
  982.6 22.9 %collective-permute-done.2 = bf16[2,640,384]{2,1,0:T(8,128)(2,1)} collective-permute-done((bf16[2,640,384]{2,1,0:T(8,128)(2,1)S(1)}, bf16[2,640,384]{2,1,0:T(8,128)(2,1)}, u32[]{:S(2)}, u32[]{:S(2)}) %collective-permute-start.2) | collective-permute-done | bytes 983072 | tf_op jit(solution)/shard_map/while/body/eval_jaxpr/ppermute | solution.py:17
  1019.7 128.4 %while.79 = (s32[]{:T(128)}, f32[2,640,384]{2,1,0:T(8,128)}, f32[5,2,640,384]{3,2,1,0:T(8,128)}, s32[]{:T(128)}, s32[]{:T(128)}) while((s32[]{:T(128)}, f32[2,640,384]{2,1,0:T(8,128)}, f32[5,2,640,384]{3,2,1,0:T(8,128)}, s32[]{:T(128)}, s32[]{:T(128)}) %tuple.144), condition=%wide.region_25.26_spmd.clone, body=%wide.region_24.25_spmd.clone.sunk | while | flops 1966083 | bytes 11796595 | solution.py:203
  1229.0 82.0 %all-reduce = (f32[384]{0:T(512)}, f32[2,32]{1,0:T(2,128)S(1)}, f32[1536]{0:T(1024)}, f32[384]{0:T(512)}) all-reduce(f32[384]{0:T(512)S(1)} %convert_reduce_fusion.6, bf16[2,32]{1,0:T(2,128)(2,1)S(1)} %copy.95, f32[1536]{0:T(1024)S(1)} %get-tuple-element.395, f32[384]{0:T(512)S(1)} %get-tuple-element.414), channel_id=1, replica_groups=mesh['seq'=16,'head'=2] {'seq'}, use_global_device_ids=true, to_apply=%region_33.34 | all-reduce | flops 2368 | bytes 18816 | tf_op jit(solution)/shard_map/psum | solution.py:233
  1313.5 306.4 %all-reduce.4.cloned.1.call-done = (f32[768,3,384]{2,0,1:T(8,128)}, f32[768,1536]{1,0:T(8,128)}, f32[384,768]{1,0:T(8,128)}, f32[1536,768]{1,0:T(8,128)}) async-done(((f32[768,3,384]{2,0,1:T(8,128)}, f32[768,1536]{1,0:T(8,128)}, f32[384,768]{1,0:T(8,128)}, f32[1536,768]{1,0:T(8,128)}), (f32[768,3,384]{2,0,1:T(8,128)}, f32[768,1536]{1,0:T(8,128)}, f32[384,768]{1,0:T(8,128)}, ...) | async-done | bytes 14155792 | tf_op jit(solution)/shard_map/psum | solution.py:233
  (606 shorter events, 871.7 us)
Async XLA Ops:
  8.0 1210.8 %reduce-scatter.19.cloned.1.call-start = ((), (), s32[]{:S(2)}) async-start(), calls=%async_computation.7 | async-start | bytes 24576
  36.0 26.4 %collective-permute-start = (bf16[2,640,384]{2,1,0:T(8,128)(2,1)}, bf16[2,640,384]{2,1,0:T(8,128)(2,1)}, u32[]{:S(2)}, u32[]{:S(2)}) collective-permute-start(bf16[2,640,384]{2,1,0:T(8,128)(2,1)} %get-tuple-element.650), channel_id=1, source_target_pairs={{0,2},{2,4},{4,6},{6,8},{8,10},{10,12},{12,14},{14,16},{16,18},{18... | collective-permute-start | bytes 2949128 | tf_op jit(solution)/shard_map/while/body/eval_jaxpr/ppermute | solution.py:17
  69.1 25.1 %collective-permute-start = (bf16[2,640,384]{2,1,0:T(8,128)(2,1)}, bf16[2,640,384]{2,1,0:T(8,128)(2,1)}, u32[]{:S(2)}, u32[]{:S(2)}) collective-permute-start(bf16[2,640,384]{2,1,0:T(8,128)(2,1)} %get-tuple-element.650), channel_id=1, source_target_pairs={{0,2},{2,4},{4,6},{6,8},{8,10},{10,12},{12,14},{14,16},{16,18},{18... | collective-permute-start | bytes 2949128 | tf_op jit(solution)/shard_map/while/body/eval_jaxpr/ppermute | solution.py:17
  100.9 24.3 %collective-permute-start = (bf16[2,640,384]{2,1,0:T(8,128)(2,1)}, bf16[2,640,384]{2,1,0:T(8,128)(2,1)}, u32[]{:S(2)}, u32[]{:S(2)}) collective-permute-start(bf16[2,640,384]{2,1,0:T(8,128)(2,1)} %get-tuple-element.650), channel_id=1, source_target_pairs={{0,2},{2,4},{4,6},{6,8},{8,10},{10,12},{12,14},{14,16},{16,18},{18... | collective-permute-start | bytes 2949128 | tf_op jit(solution)/shard_map/while/body/eval_jaxpr/ppermute | solution.py:17
  131.9 24.2 %collective-permute-start = (bf16[2,640,384]{2,1,0:T(8,128)(2,1)}, bf16[2,640,384]{2,1,0:T(8,128)(2,1)}, u32[]{:S(2)}, u32[]{:S(2)}) collective-permute-start(bf16[2,640,384]{2,1,0:T(8,128)(2,1)} %get-tuple-element.650), channel_id=1, source_target_pairs={{0,2},{2,4},{4,6},{6,8},{8,10},{10,12},{12,14},{14,16},{16,18},{18... | collective-permute-start | bytes 2949128 | tf_op jit(solution)/shard_map/while/body/eval_jaxpr/ppermute | solution.py:17
  162.9 23.5 %collective-permute-start = (bf16[2,640,384]{2,1,0:T(8,128)(2,1)}, bf16[2,640,384]{2,1,0:T(8,128)(2,1)}, u32[]{:S(2)}, u32[]{:S(2)}) collective-permute-start(bf16[2,640,384]{2,1,0:T(8,128)(2,1)} %get-tuple-element.650), channel_id=1, source_target_pairs={{0,2},{2,4},{4,6},{6,8},{8,10},{10,12},{12,14},{14,16},{16,18},{18... | collective-permute-start | bytes 2949128 | tf_op jit(solution)/shard_map/while/body/eval_jaxpr/ppermute | solution.py:17
  195.9 23.4 %collective-permute-start.1 = (bf16[2,640,384]{2,1,0:T(8,128)(2,1)}, bf16[2,640,384]{2,1,0:T(8,128)(2,1)}, u32[]{:S(2)}, u32[]{:S(2)}) collective-permute-start(bf16[2,640,384]{2,1,0:T(8,128)(2,1)} %get-tuple-element.638), channel_id=1, source_target_pairs={{2,0},{4,2},{6,4},{8,6},{10,8},{12,10},{14,12},{16,14},{18,16},{20... | collective-permute-start | bytes 2949128 | tf_op jit(solution)/shard_map/while/body/eval_jaxpr/ppermute | solution.py:17
  226.0 22.8 %collective-permute-start.1 = (bf16[2,640,384]{2,1,0:T(8,128)(2,1)}, bf16[2,640,384]{2,1,0:T(8,128)(2,1)}, u32[]{:S(2)}, u32[]{:S(2)}) collective-permute-start(bf16[2,640,384]{2,1,0:T(8,128)(2,1)} %get-tuple-element.638), channel_id=1, source_target_pairs={{2,0},{4,2},{6,4},{8,6},{10,8},{12,10},{14,12},{16,14},{18,16},{20... | collective-permute-start | bytes 2949128 | tf_op jit(solution)/shard_map/while/body/eval_jaxpr/ppermute | solution.py:17
  255.5 22.1 %collective-permute-start.1 = (bf16[2,640,384]{2,1,0:T(8,128)(2,1)}, bf16[2,640,384]{2,1,0:T(8,128)(2,1)}, u32[]{:S(2)}, u32[]{:S(2)}) collective-permute-start(bf16[2,640,384]{2,1,0:T(8,128)(2,1)} %get-tuple-element.638), channel_id=1, source_target_pairs={{2,0},{4,2},{6,4},{8,6},{10,8},{12,10},{14,12},{16,14},{18,16},{20... | collective-permute-start | bytes 2949128 | tf_op jit(solution)/shard_map/while/body/eval_jaxpr/ppermute | solution.py:17
  284.3 22.5 %collective-permute-start.1 = (bf16[2,640,384]{2,1,0:T(8,128)(2,1)}, bf16[2,640,384]{2,1,0:T(8,128)(2,1)}, u32[]{:S(2)}, u32[]{:S(2)}) collective-permute-start(bf16[2,640,384]{2,1,0:T(8,128)(2,1)} %get-tuple-element.638), channel_id=1, source_target_pairs={{2,0},{4,2},{6,4},{8,6},{10,8},{12,10},{14,12},{16,14},{18,16},{20... | collective-permute-start | bytes 2949128 | tf_op jit(solution)/shard_map/while/body/eval_jaxpr/ppermute | solution.py:17
  313.6 20.4 %collective-permute-start.1 = (bf16[2,640,384]{2,1,0:T(8,128)(2,1)}, bf16[2,640,384]{2,1,0:T(8,128)(2,1)}, u32[]{:S(2)}, u32[]{:S(2)}) collective-permute-start(bf16[2,640,384]{2,1,0:T(8,128)(2,1)} %get-tuple-element.638), channel_id=1, source_target_pairs={{2,0},{4,2},{6,4},{8,6},{10,8},{12,10},{14,12},{16,14},{18,16},{20... | collective-permute-start | bytes 2949128 | tf_op jit(solution)/shard_map/while/body/eval_jaxpr/ppermute | solution.py:17
  856.2 27.0 %collective-permute-start.2 = (bf16[2,640,384]{2,1,0:T(8,128)(2,1)S(1)}, bf16[2,640,384]{2,1,0:T(8,128)(2,1)}, u32[]{:S(2)}, u32[]{:S(2)}) collective-permute-start(bf16[2,640,384]{2,1,0:T(8,128)(2,1)S(1)} %fusion.170), channel_id=1, source_target_pairs={{2,0},{4,2},{6,4},{8,6},{10,8},{12,10},{14,12},{16,14},{18,16},{20... | collective-permute-start | bytes 2949128 | tf_op jit(solution)/shard_map/while/body/eval_jaxpr/ppermute | solution.py:17
  888.3 26.7 %collective-permute-start.2 = (bf16[2,640,384]{2,1,0:T(8,128)(2,1)S(1)}, bf16[2,640,384]{2,1,0:T(8,128)(2,1)}, u32[]{:S(2)}, u32[]{:S(2)}) collective-permute-start(bf16[2,640,384]{2,1,0:T(8,128)(2,1)S(1)} %fusion.170), channel_id=1, source_target_pairs={{2,0},{4,2},{6,4},{8,6},{10,8},{12,10},{14,12},{16,14},{18,16},{20... | collective-permute-start | bytes 2949128 | tf_op jit(solution)/shard_map/while/body/eval_jaxpr/ppermute | solution.py:17
  919.9 26.4 %collective-permute-start.2 = (bf16[2,640,384]{2,1,0:T(8,128)(2,1)S(1)}, bf16[2,640,384]{2,1,0:T(8,128)(2,1)}, u32[]{:S(2)}, u32[]{:S(2)}) collective-permute-start(bf16[2,640,384]{2,1,0:T(8,128)(2,1)S(1)} %fusion.170), channel_id=1, source_target_pairs={{2,0},{4,2},{6,4},{8,6},{10,8},{12,10},{14,12},{16,14},{18,16},{20... | collective-permute-start | bytes 2949128 | tf_op jit(solution)/shard_map/while/body/eval_jaxpr/ppermute | solution.py:17
  951.4 25.0 %collective-permute-start.2 = (bf16[2,640,384]{2,1,0:T(8,128)(2,1)S(1)}, bf16[2,640,384]{2,1,0:T(8,128)(2,1)}, u32[]{:S(2)}, u32[]{:S(2)}) collective-permute-start(bf16[2,640,384]{2,1,0:T(8,128)(2,1)S(1)} %fusion.170), channel_id=1, source_target_pairs={{2,0},{4,2},{6,4},{8,6},{10,8},{12,10},{14,12},{16,14},{18,16},{20... | collective-permute-start | bytes 2949128 | tf_op jit(solution)/shard_map/while/body/eval_jaxpr/ppermute | solution.py:17
  981.3 24.2 %collective-permute-start.2 = (bf16[2,640,384]{2,1,0:T(8,128)(2,1)S(1)}, bf16[2,640,384]{2,1,0:T(8,128)(2,1)}, u32[]{:S(2)}, u32[]{:S(2)}) collective-permute-start(bf16[2,640,384]{2,1,0:T(8,128)(2,1)S(1)} %fusion.170), channel_id=1, source_target_pairs={{2,0},{4,2},{6,4},{8,6},{10,8},{12,10},{14,12},{16,14},{18,16},{20... | collective-permute-start | bytes 2949128 | tf_op jit(solution)/shard_map/while/body/eval_jaxpr/ppermute | solution.py:17
  1021.5 22.5 %collective-permute-start.3 = (bf16[2,640,384]{2,1,0:T(8,128)(2,1)S(1)}, bf16[2,640,384]{2,1,0:T(8,128)(2,1)}, u32[]{:S(2)}, u32[]{:S(2)}) collective-permute-start(bf16[2,640,384]{2,1,0:T(8,128)(2,1)S(1)} %fusion.171), channel_id=1, source_target_pairs={{0,2},{2,4},{4,6},{6,8},{8,10},{10,12},{12,14},{14,16},{16,18},{18... | collective-permute-start | bytes 2949128 | tf_op jit(solution)/shard_map/while/body/eval_jaxpr/ppermute | solution.py:17
  1048.9 21.3 %collective-permute-start.3 = (bf16[2,640,384]{2,1,0:T(8,128)(2,1)S(1)}, bf16[2,640,384]{2,1,0:T(8,128)(2,1)}, u32[]{:S(2)}, u32[]{:S(2)}) collective-permute-start(bf16[2,640,384]{2,1,0:T(8,128)(2,1)S(1)} %fusion.171), channel_id=1, source_target_pairs={{0,2},{2,4},{4,6},{6,8},{8,10},{10,12},{12,14},{14,16},{16,18},{18... | collective-permute-start | bytes 2949128 | tf_op jit(solution)/shard_map/while/body/eval_jaxpr/ppermute | solution.py:17
  1075.2 21.0 %collective-permute-start.3 = (bf16[2,640,384]{2,1,0:T(8,128)(2,1)S(1)}, bf16[2,640,384]{2,1,0:T(8,128)(2,1)}, u32[]{:S(2)}, u32[]{:S(2)}) collective-permute-start(bf16[2,640,384]{2,1,0:T(8,128)(2,1)S(1)} %fusion.171), channel_id=1, source_target_pairs={{0,2},{2,4},{4,6},{6,8},{8,10},{10,12},{12,14},{14,16},{16,18},{18... | collective-permute-start | bytes 2949128 | tf_op jit(solution)/shard_map/while/body/eval_jaxpr/ppermute | solution.py:17
  1101.2 20.1 %collective-permute-start.3 = (bf16[2,640,384]{2,1,0:T(8,128)(2,1)S(1)}, bf16[2,640,384]{2,1,0:T(8,128)(2,1)}, u32[]{:S(2)}, u32[]{:S(2)}) collective-permute-start(bf16[2,640,384]{2,1,0:T(8,128)(2,1)S(1)} %fusion.171), channel_id=1, source_target_pairs={{0,2},{2,4},{4,6},{6,8},{8,10},{10,12},{12,14},{14,16},{16,18},{18... | collective-permute-start | bytes 2949128 | tf_op jit(solution)/shard_map/while/body/eval_jaxpr/ppermute | solution.py:17
  1158.5 61.2 %reduce-scatter.17.cloned.1.call-start = ((), (), s32[]{:S(2)}) async-start(), calls=%async_computation.6 | async-start | bytes 294912
  1185.3 35.4 %reduce-scatter.15.cloned.1.call-start = ((), (), s32[]{:S(2)}) async-start(), calls=%async_computation.5 | async-start | bytes 1474560
  1191.2 33.8 %reduce-scatter.13.cloned.1.call-start = ((), (), s32[]{:S(2)}) async-start(), calls=%async_computation.4 | async-start | bytes 1474560
  1201.7 418.2 %all-reduce.4.cloned.1.call-start = ((), (), s32[]{:S(2)}) async-start(), calls=%async_computation.8 | async-start | bytes 28311552 | tf_op jit(solution)/shard_map/psum | solution.py:233
  (89 other events, 2759.4 us)
Sparse Core Ops, SparseCore 0:
  1158.6 15.9 reduce-scatter.18
  1185.5 16.0 reduce-scatter.16
  1203.8 9.4 reduce-scatter.14
  1215.4 9.5 reduce-scatter.12
Sparse Core Ops, SparseCore 1:
  1218.9 400.9 all-reduce.3
where the time goes:
time: 1650 us; the launch traced here: 1640 us
  waiting for transfers between devices  705 us (43%)
  matrix products  357 us (22%)
  local copies, waits for them, and re-layouts  246 us (15%)
  other arithmetic  138 us (8%)
  blocking collectives  87.8 us (5%)
  starting transfers between devices  72.7 us (4%)
    ppermute x20, waiting for transfers between devices, from_behind(): return lax.ppermute(block, axis, route)  396 us
    psum x1, waiting for transfers between devices, on_device(): lax.psum((grad_qkv, grad_up, grad_attn_out, grad_down, grad_up_bias, grad...  306 us
    dot_general x11, matrix products, online_update(): jnp.einsum('hqk,khc->qhc', probs.astype(jnp.bfloat16), kv_block[1].reshap...  83.9 us
    psum x1, blocking collectives, on_device(): lax.psum((grad_qkv, grad_up, grad_attn_out, grad_down, grad_up_bias, grad...  82 us
    dot_general x22, matrix products, head_scores(): jnp.einsum('qhc,khc->hqk', queries, key_part, preferred_element_type=jnp....  74.6 us
    ppermute x20, starting transfers between devices, from_behind(): return lax.ppermute(block, axis, route)  72.3 us
    dot_general x11, matrix products, grad_update(): jnp.einsum('hqk,khc->qhc', d_scores, key_part, preferred_element_type=jnp...  50 us
    while x65, local copies, waits for them, and re-layouts  47.6 us
  transfers between devices with their start and end apart: 25, of which 22 were waited for; matrix products, arithmetic and copies ran while one was open for 4% of the time, Pallas kernels for 0%

commit v1 on v0

v1 whole, which is shorter than its diff:
```python
import functools

import jax
import jax.numpy as jnp
from jax import lax
from jax.experimental import pallas as pl
from jax.experimental.pallas import tpu as pltpu
from jax.sharding import PartitionSpec as P

HS = 64
LONG_LEN = 3136
EPSILON = 1e-06
F32 = jnp.float32
BF16 = jnp.bfloat16
TILE = 256
VMEM_LIMIT = 60 * 1024 * 1024


def layer_norm(values, gain_row):
    row_mean = jnp.mean(values, axis=-1, keepdims=True)
    centred = values - row_mean
    spread = jnp.mean(centred * centred, axis=-1, keepdims=True)
    return centred * lax.rsqrt(spread + EPSILON) * gain_row


def exact_gelu(values):
    return jax.nn.gelu(values, approximate=False)


def dot_nn(a, b):
    return lax.dot_general(a, b, (((1,), (0,)), ((), ())), preferred_element_type=F32)


def dot_nt(a, b):
    return lax.dot_general(a, b, (((1,), (1,)), ((), ())), preferred_element_type=F32)


def dot_tn(a, b):
    return lax.dot_general(a, b, (((0,), (0,)), ((), ())), preferred_element_type=F32)


def half_means(block):
    left = lax.broadcasted_iota(jnp.int32, (128, 128), 0) // HS
    right = lax.broadcasted_iota(jnp.int32, (128, 128), 1) // HS
    averager = jnp.where(left == right, 1.0 / HS, 0.0).astype(F32)
    return lax.dot_general(
        block,
        averager,
        (((1,), (0,)), ((), ())),
        precision=lax.Precision.HIGHEST,
        preferred_element_type=F32,
    )


def normalized_halves(block):
    centred = block - half_means(block)
    inverse = lax.rsqrt(half_means(centred * centred) + EPSILON)
    return centred * inverse, inverse


def work_table(image_starts, place, n_seq, tok_rows, reach):
    window = reach + 1
    total = n_seq * tok_rows
    candidates = jnp.arange(2 * reach, dtype=jnp.int32) + place - reach
    positions = jnp.concatenate(
        [(candidates + 1) * tok_rows - 1, jnp.stack([place * tok_rows, (place + 1) * tok_rows - 1])]
    )
    below = image_starts[None, :] <= positions[:, None]
    starts = jnp.max(jnp.where(below, image_starts[None, :], -1), axis=1)
    ends = jnp.min(jnp.where(below, total, image_starts[None, :]), axis=1)
    first = starts // tok_rows
    last = (ends - 1) // tok_rows
    base = jnp.minimum(first, n_seq - window)
    spans = last > first
    mine = (
        (candidates >= 0)
        & (candidates < n_seq)
        & (first[:-2] == candidates)
        & spans[:-2]
        & (base[:-2] <= place)
        & (base[:-2] >= place - reach)
    )
    lengths = jnp.where(mine, ends[:-2] - starts[:-2], 0)
    rows = jnp.where(mine, starts[:-2] - (place - reach) * tok_rows, 0)
    low_end = jnp.where(spans[-2], jnp.clip(ends[-2] - place * tok_rows, 0, tok_rows), 0)
    low_end = jnp.where(first[-2] < place, low_end, 0)
    high_start = jnp.clip(starts[-1] - place * tok_rows, 0, tok_rows)
    high_start = jnp.where(last[-1] > place, high_start, tok_rows)
    head_part = jnp.stack([low_end, high_start, place - base[-2], place - base[-1]])
    return jnp.concatenate([head_part, rows, lengths]).astype(jnp.int32)


def pack_kernel(heads, reach, table, proj, datt, gains, *outs):
    slots, local = outs[:-1], outs[-1]
    rows = proj.shape[1]
    low = lax.broadcasted_iota(jnp.int32, (rows, 128), 1) < HS
    q_gain = gains[0:1, :] * (HS**-0.5)
    k_gain = gains[1:2, :]
    for pair in range(heads // 2):
        lanes = slice(pair * 128, (pair + 1) * 128)
        q = normalized_halves(proj[0, :, lanes])[0] * q_gain
        k = normalized_halves(proj[1, :, lanes])[0] * k_gain
        v = proj[2, :, lanes]
        d = datt[:, lanes].astype(F32)
        q, k, v = (t.astype(BF16).astype(F32) for t in (q, k, v))
        local[2 * pair, :, 0:128] = jnp.where(low, q, pltpu.roll(k, HS, 1)).astype(BF16)
        local[2 * pair, :, 128:256] = jnp.where(low, v, pltpu.roll(d, HS, 1)).astype(BF16)
        local[2 * pair + 1, :, 0:128] = jnp.where(low, pltpu.roll(q, HS, 1), k).astype(BF16)
        local[2 * pair + 1, :, 128:256] = jnp.where(low, pltpu.roll(v, HS, 1), d).astype(BF16)
    low_end = table[0]
    from_low = lax.broadcasted_iota(jnp.int32, (rows, 256), 0) < low_end
    for index, slot in enumerate(slots):
        distance = index - reach
        low_head = jnp.clip(table[2] + distance, 0, heads - 1)
        high_head = jnp.clip(table[3] + distance, 0, heads - 1)
        picked = jnp.where(from_low, local[low_head].astype(F32), local[high_head].astype(F32))
        slot[...] = picked.astype(BF16)


def softmax_tail(mixed, d_out):
    lane = lax.broadcasted_iota(jnp.int32, mixed.shape, 1)
    total = mixed[:, HS : HS + 1]
    inverse = 1.0 / jnp.where(total > 0, total, 1.0)
    mixture = mixed * inverse
    delta = jnp.sum(d_out * mixture, axis=1, keepdims=True)
    shift = -delta * inverse
    coarse = shift.astype(BF16).astype(F32)
    scaled = jnp.where(lane == HS, coarse, jnp.where(lane == HS + 1, shift - coarse, d_out * inverse))
    return mixture, scaled.astype(BF16)


def work_kernel(reach, tok_rows, max_tiles, table, *refs):
    count = 2 * reach + 1
    inputs, outputs = refs[:count], refs[count : 2 * count]
    x, y, qb, kb, vb, db, eb, dk, dv, in_sem, out_sem = refs[2 * count :]

    def copy_in(b):
        return pltpu.make_async_copy(inputs[b], x.at[pl.ds(b * tok_rows, tok_rows)], in_sem.at[b])

    def copy_out(b):
        return pltpu.make_async_copy(y.at[pl.ds(b * tok_rows, tok_rows)], outputs[b], out_sem.at[b])

    for b in range(count):
        copy_in(b).start()
    for b in range(count):
        copy_in(b).wait()
    row = lax.broadcasted_iota(jnp.int32, (TILE, 128), 0)
    lane = lax.broadcasted_iota(jnp.int32, (TILE, 128), 1)
    low = lane < HS

    @pl.loop(0, 2 * reach)
    def _(job):
        length = table[4 + 2 * reach + job]
        first = table[4 + job]
        aligned = pl.multiple_of((first // 16) * 16, 16)
        lead = first - aligned
        tiles = (lead + length + TILE - 1) // TILE
        tiles = jnp.where(length > 0, tiles, 0)

        def inside(t):
            at = row + t * TILE
            return (at >= lead) & (at < lead + length)

        @pl.loop(0, tiles)
        def _(t):
            at = pl.multiple_of(t * TILE, TILE)
            source = pl.ds(aligned + at, TILE)
            ours = inside(t)
            keep = low & ours
            qk = x[source, 0:128].astype(F32)
            vd = x[source, 128:256].astype(F32)
            ones = jnp.where(lane < HS + 2, 1.0, 0.0)
            qb[pl.ds(at, TILE), :] = jnp.where(keep, qk, 0.0).astype(BF16)
            kb[pl.ds(at, TILE), :] = jnp.where(keep, pltpu.roll(qk, HS, 1), 0.0).astype(BF16)
            vb[pl.ds(at, TILE), :] = jnp.where(ours, jnp.where(low, vd, ones), 0.0).astype(BF16)
            db[pl.ds(at, TILE), :] = jnp.where(keep, pltpu.roll(vd, HS, 1), 0.0).astype(BF16)
            dk[:, pl.ds(at, TILE)] = jnp.zeros((HS, TILE), F32)
            dv[:, pl.ds(at, TILE)] = jnp.zeros((HS, TILE), F32)

        def store(t, lanes, value):
            place = pl.ds(aligned + pl.multiple_of(t * TILE, TILE), TILE)
            old = y[place, lanes].astype(F32)
            y[place, lanes] = jnp.where(inside(t), value, old).astype(BF16)

        def first_pass(q, at):
            e = jnp.exp(dot_nt(q, kb[at, :])).astype(BF16)
            eb[:, at] = e

        def second_pass(q, scaled, at):
            e = eb[:, at]
            dv[:, at] += dot_tn(scaled[:, :HS], e)
            grad = dot_nt(scaled, vb[at, :])
            ds = (e.astype(F32) * grad).astype(BF16)
            eb[:, at] = ds
            dk[:, at] += dot_tn(q[:, :HS], ds)

        @pl.when(tiles == max_tiles)
        def _():
            @pl.loop(0, max_tiles)
            def _(t):
                at = pl.ds(pl.multiple_of(t * TILE, TILE), TILE)
                q = qb[at, :]
                for s in range(max_tiles):
                    first_pass(q, slice(s * TILE, (s + 1) * TILE))
                mixture, scaled = softmax_tail(dot_nn(eb[...], vb[...]), db[at, :].astype(F32))
                for s in range(max_tiles):
                    second_pass(q, scaled, slice(s * TILE, (s + 1) * TILE))
                d_query = dot_nn(eb[...], kb[...])
                store(t, slice(0, 128), jnp.where(low, mixture, pltpu.roll(d_query, HS, 1)))

        @pl.when((tiles > 0) & (tiles < max_tiles))
        def _():
            @pl.loop(0, tiles)
            def _(t):
                at = pl.ds(pl.multiple_of(t * TILE, TILE), TILE)
                q = qb[at, :]

                def mix(s, total):
                    to = pl.ds(pl.multiple_of(s * TILE, TILE), TILE)
                    first_pass(q, to)
                    return total + dot_nn(eb[:, to], vb[to, :])

                mixed = lax.fori_loop(0, tiles, mix, jnp.zeros((TILE, 128), F32))
                mixture, scaled = softmax_tail(mixed, db[at, :].astype(F32))

                def back(s, total):
                    to = pl.ds(pl.multiple_of(s * TILE, TILE), TILE)
                    second_pass(q, scaled, to)
                    return total + dot_nn(eb[:, to], kb[to, :])

                d_query = lax.fori_loop(0, tiles, back, jnp.zeros((TILE, 128), F32))
                store(t, slice(0, 128), jnp.where(low, mixture, pltpu.roll(d_query, HS, 1)))

        @pl.loop(0, tiles)
        def _(t):
            at = pl.ds(pl.multiple_of(t * TILE, TILE), TILE)
            both = jnp.concatenate([dk[:, at], dv[:, at]], axis=0)
            store(t, slice(128, 256), both.T)

    for b in range(count):
        copy_out(b).start()
    for b in range(count):
        copy_out(b).wait()


def local_kernel(heads, table, local, ids_row, ids_column, out):
    rows = local.shape[1]

    @pl.when(table[0] < table[1])
    def _():
        lane = lax.broadcasted_iota(jnp.int32, (rows, 128), 1)
        low = lane < HS
        same = (ids_column[...] == ids_row[...]).astype(F32)
        ones = jnp.where(lane < HS + 2, 1.0, 0.0)

        @pl.loop(0, heads)
        def _(h):
            qk = local[h, :, 0:128].astype(F32)
            vd = local[h, :, 128:256].astype(F32)
            q = jnp.where(low, qk, 0.0).astype(BF16)
            k = jnp.where(low, pltpu.roll(qk, HS, 1), 0.0).astype(BF16)
            v = jnp.where(low, vd, ones).astype(BF16)
            d_out = jnp.where(low, pltpu.roll(vd, HS, 1), 0.0)
            e = (jnp.exp(dot_nt(q, k)) * same).astype(BF16)
            mixture, scaled = softmax_tail(dot_nn(e, v), d_out)
            ds = (e.astype(F32) * dot_nt(scaled, v)).astype(BF16)
            d_query = dot_nn(ds, k)
            d_key = dot_tn(q[:, :HS], ds)
            d_value = dot_tn(scaled[:, :HS], e)
            out[h, :, 0:128] = jnp.where(low, mixture, pltpu.roll(d_query, HS, 1)).astype(BF16)
            out[h, :, 128:256] = jnp.concatenate([d_key, d_value], axis=0).T.astype(BF16)


def unpack_kernel(heads, reach, table, proj, gains, local, *refs):
    count = 2 * reach + 1
    backs = refs[:count]
    attended, d_proj, gain_sums, stacked, sems = refs[count:]
    rows = proj.shape[1]

    def copy_in(b):
        return pltpu.make_async_copy(backs[b], stacked.at[b], sems.at[b])

    for b in range(count):
        copy_in(b).start()
    for b in range(count):
        copy_in(b).wait()
    low = lax.broadcasted_iota(jnp.int32, (rows, 128), 1) < HS
    row = lax.broadcasted_iota(jnp.int32, (rows, 256), 0)
    from_low = row < table[0]
    from_high = row >= table[1]
    q_gain = gains[0:1, :] * (HS**-0.5)
    k_gain = gains[1:2, :]

    def gathered(h):
        lower = stacked[h - table[2] + reach].astype(F32)
        upper = stacked[h - table[3] + reach].astype(F32)
        return jnp.where(from_low, lower, jnp.where(from_high, upper, local[h].astype(F32)))

    def back(raw, gradient, gain):
        hat, inverse = normalized_halves(raw)
        scaled = gradient * gain
        shifted = scaled - half_means(scaled) - hat * half_means(scaled * hat)
        return shifted * inverse, jnp.sum(gradient * hat, axis=0, keepdims=True)

    q_sum = jnp.zeros((1, 128), F32)
    k_sum = jnp.zeros((1, 128), F32)
    for pair in range(heads // 2):
        lanes = slice(pair * 128, (pair + 1) * 128)
        even, odd = gathered(2 * pair), gathered(2 * pair + 1)
        mixture = jnp.where(low, even[:, 0:128], pltpu.roll(odd[:, 0:128], HS, 1))
        d_query = jnp.where(low, pltpu.roll(even[:, 0:128], HS, 1), odd[:, 0:128])
        d_key = jnp.where(low, even[:, 128:256], pltpu.roll(odd[:, 128:256], HS, 1))
        d_value = jnp.where(low, pltpu.roll(even[:, 128:256], HS, 1), odd[:, 128:256])
        attended[:, lanes] = mixture.astype(BF16)
        q_raw, q_part = back(proj[0, :, lanes], d_query, q_gain)
        k_raw, k_part = back(proj[1, :, lanes], d_key, k_gain)
        q_sum += q_part
        k_sum += k_part
        d_proj[0, :, lanes] = q_raw.astype(BF16)
        d_proj[1, :, lanes] = k_raw.astype(BF16)
        d_proj[2, :, lanes] = d_value.astype(BF16)
    gain_sums[...] = jnp.concatenate([q_sum * (HS**-0.5), k_sum], axis=0)


def in_vmem():
    return pl.BlockSpec(memory_space=pltpu.VMEM)


def in_smem():
    return pl.BlockSpec(memory_space=pltpu.SMEM)


def anywhere():
    return pl.BlockSpec(memory_space=pl.ANY)


def compiler_params():
    return pltpu.CompilerParams(vmem_limit_bytes=VMEM_LIMIT)


def cost(flops, bytes_accessed, transcendentals=0):
    return pl.CostEstimate(
        flops=flops, bytes_accessed=bytes_accessed, transcendentals=transcendentals
    )


def pack(heads, reach, table, proj, datt, gains):
    rows = proj.shape[1]
    slot = jax.ShapeDtypeStruct((rows, 4 * HS), BF16)
    count = 2 * reach + 1
    return pl.pallas_call(
        functools.partial(pack_kernel, heads, reach),
        out_shape=[slot] * count + [jax.ShapeDtypeStruct((heads, rows, 4 * HS), BF16)],
        in_specs=[in_smem(), in_vmem(), in_vmem(), in_vmem()],
        out_specs=[in_vmem()] * (count + 1),
        compiler_params=compiler_params(),
        cost_estimate=cost(10**9, 10**7),
    )(table, proj, datt, gains)


def work(reach, tok_rows, table, blocks):
    count = 2 * reach + 1
    max_tiles = -(-(LONG_LEN + 15) // TILE)
    padded = count * tok_rows + TILE
    span = max_tiles * TILE
    return pl.pallas_call(
        functools.partial(work_kernel, reach, tok_rows, max_tiles),
        out_shape=[jax.ShapeDtypeStruct((tok_rows, 4 * HS), BF16)] * count,
        in_specs=[in_smem()] + [anywhere()] * count,
        out_specs=[anywhere()] * count,
        scratch_shapes=[
            pltpu.VMEM((padded, 4 * HS), BF16),
            pltpu.VMEM((padded, 4 * HS), BF16),
            pltpu.VMEM((span, 128), BF16),
            pltpu.VMEM((span, 128), BF16),
            pltpu.VMEM((span, 128), BF16),
            pltpu.VMEM((span, 128), BF16),
            pltpu.VMEM((TILE, span), BF16),
            pltpu.VMEM((HS, span), F32),
            pltpu.VMEM((HS, span), F32),
            pltpu.SemaphoreType.DMA((count,)),
            pltpu.SemaphoreType.DMA((count,)),
        ],
        compiler_params=compiler_params(),
        cost_estimate=cost(3 * 10**10, 10**7, 10**7),
    )(table, *blocks)


def local_work(heads, table, local, ids_row, ids_column):
    return pl.pallas_call(
        functools.partial(local_kernel, heads),
        out_shape=jax.ShapeDtypeStruct(local.shape, BF16),
        in_specs=[in_smem(), in_vmem(), in_vmem(), in_vmem()],
        out_specs=in_vmem(),
        compiler_params=compiler_params(),
        cost_estimate=cost(5 * 10**9, 4 * 10**6, 25 * 10**5),
    )(table, local, ids_row, ids_column)


def unpack(heads, reach, table, proj, gains, local, backs):
    rows = proj.shape[1]
    count = 2 * reach + 1
    width = heads * HS
    return pl.pallas_call(
        functools.partial(unpack_kernel, heads, reach),
        out_shape=[
            jax.ShapeDtypeStruct((rows, width), BF16),
            jax.ShapeDtypeStruct((3, rows, width), BF16),
            jax.ShapeDtypeStruct((2, 128), F32),
        ],
        in_specs=[in_smem(), in_vmem(), in_vmem(), in_vmem()] + [anywhere()] * count,
        out_specs=[in_vmem()] * 3,
        scratch_shapes=[
            pltpu.VMEM((count, rows, 4 * HS), BF16),
            pltpu.SemaphoreType.DMA((count,)),
        ],
        compiler_params=compiler_params(),
        cost_estimate=cost(10**9, 10**7),
    )(table, proj, gains, local, *backs)


def on_device(
    tokens,
    image_starts,
    ln_gain,
    w_qkv,
    q_gain,
    k_gain,
    w_up,
    up_bias,
    w_attn_out,
    w_down,
    out_bias,
    cotangent,
):
    tok_rows, half = tokens.shape
    local_width = w_qkv.shape[2]
    heads = local_width // HS
    reach = (LONG_LEN + tok_rows - 2) // tok_rows
    n_seq = lax.axis_size("seq")
    place = lax.axis_index("seq")
    side = lax.axis_index("head")
    assert heads == reach + 1 and n_seq >= heads and heads % 2 == 0

    def from_peer(block):
        return lax.ppermute(block, "head", [(0, 1), (1, 0)])

    def both_halves(block):
        other = from_peer(block)
        first = jnp.where(side == 0, block, other)
        second = jnp.where(side == 0, other, block)
        return jnp.concatenate([first, second], axis=1)

    def add_over_heads(partial):
        low, high = partial[:, :half], partial[:, half:]
        send = jnp.where(side == 0, high, low).astype(BF16)
        keep = jnp.where(side == 0, low, high)
        return keep + from_peer(send).astype(F32)

    def shifted(block, distance):
        if distance == 0:
            return block
        route = [(i, i + distance) for i in range(n_seq) if 0 <= i + distance < n_seq]
        return lax.ppermute(block, "seq", route)

    table = work_table(image_starts, place, n_seq, tok_rows, reach)
    row_index = jnp.arange(tok_rows, dtype=jnp.int32)
    positions = place * tok_rows + row_index
    ids = jnp.sum((image_starts[None, :] <= positions[:, None]).astype(jnp.int32), axis=1)
    is_local = (row_index >= table[0]) & (row_index < table[1])
    ids_column = jnp.where(is_local, ids, -1)[:, None]
    ids_row = jnp.where(is_local, ids, -2)[None, :]
    gains = jnp.tile(jnp.stack([q_gain, k_gain]), (1, 2))

    gathered = both_halves(tokens)
    cot_whole = both_halves(cotangent)
    normed_f, norm_pull = jax.vjp(layer_norm, gathered.astype(F32), ln_gain)
    normed = normed_f.astype(BF16)
    proj = jnp.einsum("td,dkc->ktc", normed, w_qkv, preferred_element_type=F32)
    d_attended = jnp.einsum("td,cd->tc", cot_whole, w_attn_out, preferred_element_type=F32)
    packed = pack(heads, reach, table, proj, d_attended.astype(BF16), gains)
    slots, local = packed[:-1], packed[-1]

    arrived = [shifted(slots[reach + d], d) for d in range(reach, -reach - 1, -1)]

    up_input = jnp.dot(normed, w_up, preferred_element_type=F32) + up_bias
    hidden_f, gelu_pull = jax.vjp(exact_gelu, up_input)
    hidden = hidden_f.astype(BF16)
    d_hidden = jnp.einsum("td,fd->tf", cot_whole, w_down, preferred_element_type=F32)
    d_upper_f = gelu_pull(d_hidden)[0]
    d_upper = d_upper_f.astype(BF16)
    grad_down = jnp.einsum("tf,td->fd", hidden, cot_whole, preferred_element_type=F32)
    grad_up = jnp.einsum("td,tf->df", normed, d_upper, preferred_element_type=F32)
    grad_out_bias = jnp.sum(cotangent.astype(F32), axis=0)
    grad_up_bias = jnp.sum(d_upper.astype(F32), axis=0)
    early = lax.psum((grad_down.astype(BF16), grad_up.astype(BF16)), "seq")
    ffn_out = jnp.dot(hidden, w_down, preferred_element_type=F32)
    ffn_back = jnp.einsum("tf,df->td", d_upper, w_up, preferred_element_type=F32)

    local_out = local_work(heads, table, local, ids_row, ids_column)
    worked = work(reach, tok_rows, table, arrived)
    returned = [shifted(worked[b], b - reach) for b in range(2 * reach + 1)][::-1]
    attended, d_proj, gain_sums = unpack(heads, reach, table, proj, gains, local_out, returned)

    partial_out = jnp.dot(attended, w_attn_out, preferred_element_type=F32) + ffn_out
    summed = add_over_heads(partial_out)
    block_out = (summed + tokens.astype(F32) + out_bias).astype(BF16)
    grad_attn_out = jnp.einsum("tc,td->cd", attended, cot_whole, preferred_element_type=F32)
    grad_qkv = jnp.einsum("td,ktc->dkc", normed, d_proj, preferred_element_type=F32)
    d_normed = ffn_back + jnp.einsum("ktc,dkc->td", d_proj, w_qkv, preferred_element_type=F32)
    d_input, d_ln = norm_pull(d_normed)
    input_sum = add_over_heads(d_input)
    tokens_grad = (input_sum + cotangent.astype(F32)).astype(BF16)
    gain_total = gain_sums[:, :HS] + gain_sums[:, HS:]
    small = jnp.concatenate([d_ln, gain_total.reshape(-1), grad_up_bias, grad_out_bias])
    parts = (grad_qkv.astype(BF16), grad_attn_out.astype(BF16), small[None].astype(BF16))
    parts, early = lax.optimization_barrier((parts, early))
    late = lax.psum(parts, "seq")
    sums = late[2][0].astype(F32)
    width = 2 * half
    shared = add_over_heads(sums[None, :width])[0]
    gain_pair = sums[width : width + 2 * HS].reshape(2, HS)
    gain_half = HS // 2
    gain_send = jnp.where(side == 0, gain_pair[:, gain_half:], gain_pair[:, :gain_half])
    gain_keep = jnp.where(side == 0, gain_pair[:, :gain_half], gain_pair[:, gain_half:])
    gain_grads = gain_keep + from_peer(gain_send)
    at = width + 2 * HS
    up_width = up_bias.shape[0]
    return (
        block_out,
        tokens_grad,
        shared,
        late[0].astype(F32),
        gain_grads[0],
        gain_grads[1],
        early[1].astype(F32),
        sums[at : at + up_width],
        late[1].astype(F32),
        early[0].astype(F32),
        sums[at + up_width :],
    )


def solution(mesh):
    in_specs = (
        P("seq", "head"),
        P(),
        P(),
        P(None, None, "head"),
        P(),
        P(),
        P(None, "head"),
        P("head"),
        P("head", None),
        P("head", None),
        P("head"),
        P("seq", "head"),
    )
    out_specs = (
        P("seq", "head"),
        P("seq", "head"),
        P("head"),
        P(None, None, "head"),
        P("head"),
        P("head"),
        P(None, "head"),
        P("head"),
        P("head", None),
        P("head", None),
        P("head"),
    )
    return jax.shard_map(
        on_device, mesh=mesh, in_specs=in_specs, out_specs=out_specs, check_vma=False
    )
```

time: 1650 us -> 495 us (0.30)
  waiting for transfers between devices: 705 us -> 136 us
  matrix products: 357 us -> 46.4 us
  local copies, waits for them, and re-layouts: 246 us -> 8.89 us
  other arithmetic: 138 us -> 25.3 us
  Pallas kernels: 0 us -> 88.4 us
    dot_general x89 -> x12, matrix products: 357 us -> 46.4 us  [the longest x1 9.75 us: on_device(): up_input = jnp.dot(normed, w_up, preferred_element_type=F32) + up_bias]
    ppermute x20 -> x26, waiting for transfers between devices: 396 us -> 94.3 us  [the longest x20 94.3 us: shifted(): return lax.ppermute(block, 'seq', route)]
    psum x1 -> x2, waiting for transfers between devices: 306 us -> 42.1 us  [the longest x1 42.1 us: on_device(): late = lax.psum(parts, 'seq')]
    pallas_call x0 -> x4, Pallas kernels: none -> 88.4 us  [the longest x1 47.6 us: work(): pl.pallas_call(functools.partial(work_kernel, reach, tok_rows, max_tiles)...]
    while x69 -> x0, local copies, waits for them, and re-layouts: 79.4 us -> none
    slice x24 -> x7, local copies, waits for them, and re-layouts: 52.7 us -> 4.12 us  [the longest x1 0.62 us: on_device(): sums[at:at + up_width]]
    dynamic_update_slice x20 -> x0, local copies, waits for them, and re-layouts: 44.9 us -> none  [on_device(): from_below = lax.scan(pass_up, own_block, None, length=reach_dev)[1]]
    convert_element_type x26 -> x11, other arithmetic: 58.8 us -> 15.7 us  [the longest x1 4.63 us: on_device(): early[1].astype(F32)]
  transfers between devices with their start and end apart: 25 -> 28, of which waited for: 22 -> 9; matrix products, arithmetic and copies ran while one was open for 4% -> 13% of each run, Pallas kernels for 0% -> 16%
where the time goes in v1:
time: 495 us; the launch traced here: 493 us
  waiting for transfers between devices  136 us (27%)
  Pallas kernels  88.4 us (18%)
  blocking collectives  85.5 us (17%)
  starting transfers between devices  82.4 us (17%)
  matrix products  46.4 us (9%)
  other arithmetic  25.3 us (5%)
  between operations  19.4 us (4%)
  local copies, waits for them, and re-layouts  8.89 us (2%)
    ppermute x20, waiting for transfers between devices, shifted(): return lax.ppermute(block, 'seq', route)  94.3 us
    psum x1, blocking collectives, on_device(): late = lax.psum(parts, 'seq')  85.5 us
    ppermute x20, starting transfers between devices, shifted(): return lax.ppermute(block, 'seq', route)  80.5 us
    pallas_call x1, Pallas kernels, work(): pl.pallas_call(functools.partial(work_kernel, reach, tok_rows, max_tiles)...  47.6 us
    psum x1, waiting for transfers between devices, on_device(): late = lax.psum(parts, 'seq')  42.1 us
    pallas_call x1, Pallas kernels, local_work(): pl.pallas_call(functools.partial(local_kernel, heads), out_shape=jax.Shap...  18.2 us
    pallas_call x1, Pallas kernels, unpack(): pl.pallas_call(functools.partial(unpack_kernel, heads, reach), out_shape=...  13.6 us
  transfers between devices with their start and end apart: 28, of which 9 were waited for; matrix products, arithmetic and copies ran while one was open for 13% of the time, Pallas kernels for 16%

profile of v1, /device:TPU:0, one launch (start us, length us, event | category | flops | bytes accessed | tf_op | source)
XLA Modules:
  0.0 492.6 jit_solution(13766572664618102916)
XLA Ops:
  29.9 8.9 %shard_map.203 = (bf16[640,256]{1,0:T(8,128)(2,1)}, bf16[640,256]{1,0:T(8,128)(2,1)}, bf16[640,256]{1,0:T(8,128)(2,1)}, bf16[640,256]{1,0:T(8,128)(2,1)}, bf16[6...) custom-call(s32[24]{0:T(128)} %concatenate.32.table, ...), custom_call_target="tpu_custom_call" | custom-call | flops 1000000000 | bytes 10000000 | tf_op jit(solution)/shard_map/pallas_call | solution.py:351
  38.9 6.5 %collective-permute-start.2 = (bf16[640,256]{1,0:T(8,128)(2,1)}, bf16[640,256]{1,0:T(8,128)(2,1)}, u32[]{:S(2)}, u32[]{:S(2)}) collective-permute-start(bf16[640,256]{1,0:T(8,128)(2,1)} %get-tuple-element.43), channel_id=1, source_target_pairs={{0,10},{2,12},{4,14},{6,16},{8,18},{10,20},{12,22},{14,24},{16,26}... | collective-permute-start | bytes 983048 | tf_op jit(solution)/shard_map/ppermute | solution.py:464
  45.4 4.2 collective-permute-start.3
  49.6 4.4 collective-permute-start.4
  60.5 9.8 %multiply_convert_fusion = (bf16[640,1536]{1,0:T(8,128)(2,1)S(1)}, f32[640,1536]{1,0:T(8,128)S(1)}, f32[640,1536]{1,0:T(8,128)S(1)}) fusion(f32[1536]{0:T(1024)S(1)} %copy-done.24, bf16[768,1536]{1,0:T(8,128)(2,1)S(1)} %copy-done, f32[768]{0:T(1024)S(1)} %copy-done.18, f32[640]{0:T(1024)S(1)} %fusion.21, f32[640]{0:T(1024)S(1)} %broadcast_multiply_fusion, ...), kind=kOutput, calls=%fused_computation.3 | convolution fusion | flops 1578762240 | bytes 13187072 | tf_op jit(solution)/shard_map/dot_general | solution.py:486
  70.3 3.7 fusion.35
  74.0 3.6 convolution_convert_fusion
  87.7 5.3 %fusion.36 = f32[640,768]{1,0:T(8,128)} fusion(bf16[640,1536]{1,0:T(8,128)(2,1)} %copy-done.25, bf16[1536,768]{1,0:T(8,128)(2,1)} %param.21), kind=kOutput, calls=%fused_computation.97 | convolution fusion | flops 1509949440 | bytes 6291456 | tf_op jit(solution)/shard_map/dot_general | solution.py:497
  93.0 7.0 %collective-permute-done.7.refs_6_ = bf16[640,256]{1,0:T(8,128)(2,1)S(1)} collective-permute-done((bf16[640,256]{1,0:T(8,128)(2,1)}, bf16[640,256]{1,0:T(8,128)(2,1)S(1)}, u32[]{:S(2)}, u32[]{:S(2)}) %collective-permute-start.7) | collective-permute-done | bytes 327712 | tf_op jit(solution)/shard_map/ppermute | solution.py:464
  100.0 7.8 %collective-permute-done.8.refs_7_ = bf16[640,256]{1,0:T(8,128)(2,1)} collective-permute-done((bf16[640,256]{1,0:T(8,128)(2,1)}, bf16[640,256]{1,0:T(8,128)(2,1)}, u32[]{:S(2)}, u32[]{:S(2)}) %collective-permute-start.8) | collective-permute-done | bytes 327712 | tf_op jit(solution)/shard_map/ppermute | solution.py:464
  110.3 39.1 %collective-permute-done.10.refs_9_ = bf16[640,256]{1,0:T(8,128)(2,1)} collective-permute-done((bf16[640,256]{1,0:T(8,128)(2,1)}, bf16[640,256]{1,0:T(8,128)(2,1)}, u32[]{:S(2)}, u32[]{:S(2)}) %collective-permute-start.10) | collective-permute-done | bytes 327712 | tf_op jit(solution)/shard_map/ppermute | solution.py:464
  151.9 47.6 %shard_map.205 = (bf16[640,256]{1,0:T(8,128)(2,1)}, bf16[640,256]{1,0:T(8,128)(2,1)}, bf16[640,256]{1,0:T(8,128)(2,1)}, bf16[640,256]{1,0:T(8,128)(2,1)}, bf16[6...) custom-call(s32[24]{0:T(128)} %concatenate.32.table, ...), custom_call_target="tpu_custom_call" | custom-call | flops 30000001024 | bytes 10000000 | tf_op jit(solution)/shard_map/pallas_call | solution.py:366
  202.5 8.6 %collective-permute-start.13 = (bf16[640,256]{1,0:T(8,128)(2,1)}, bf16[640,256]{1,0:T(8,128)(2,1)}, u32[]{:S(2)}, u32[]{:S(2)}) collective-permute-start(bf16[640,256]{1,0:T(8,128)(2,1)} %get-tuple-element.55), channel_id=1, source_target_pairs={{0,8},{2,10},{4,12},{6,14},{8,16},{10,18},{12,20},{14,22},{16,24},... | collective-permute-start | bytes 983048 | tf_op jit(solution)/shard_map/ppermute | solution.py:464
  211.2 13.4 %collective-permute-start.14 = (bf16[640,256]{1,0:T(8,128)(2,1)}, bf16[640,256]{1,0:T(8,128)(2,1)}, u32[]{:S(2)}, u32[]{:S(2)}) collective-permute-start(bf16[640,256]{1,0:T(8,128)(2,1)} %get-tuple-element.56), channel_id=1, source_target_pairs={{0,6},{2,8},{4,10},{6,12},{8,14},{10,16},{12,18},{14,20},{16,22},{... | collective-permute-start | bytes 983048 | tf_op jit(solution)/shard_map/ppermute | solution.py:464
  224.6 19.0 %collective-permute-start.15 = (bf16[640,256]{1,0:T(8,128)(2,1)}, bf16[640,256]{1,0:T(8,128)(2,1)}, u32[]{:S(2)}, u32[]{:S(2)}) collective-permute-start(bf16[640,256]{1,0:T(8,128)(2,1)} %get-tuple-element.57), channel_id=1, source_target_pairs={{0,4},{2,6},{4,8},{6,10},{8,12},{10,14},{12,16},{14,18},{16,20},{1... | collective-permute-start | bytes 983048 | tf_op jit(solution)/shard_map/ppermute | solution.py:464
  245.5 4.5 fusion.37
  256.7 18.2 %shard_map.204.local = bf16[6,640,256]{2,1,0:T(8,128)(2,1)} custom-call(s32[24]{0:T(128)} %concatenate.32.table, bf16[6,640,256]{2,1,0:T(8,128)(2,1)} %get-tuple-element.42.local, s32[1,640]{1,0:T(1,128)} %and_select_fusion.ids_row, s32[640,1]{1,0:T(8,128)} %reshape_select_fusion.ids_column), custom_call_target="tpu_custom_call" | custom-call | flops 5000000000 | bytes 4000000 | tf_op jit(solution)/shard_map/pallas_call | solution.py:390
  275.0 23.8 %collective-permute-done.20.refs_9_ = bf16[640,256]{1,0:T(8,128)(2,1)} collective-permute-done((bf16[640,256]{1,0:T(8,128)(2,1)}, bf16[640,256]{1,0:T(8,128)(2,1)}, u32[]{:S(2)}, u32[]{:S(2)}) %collective-permute-start.20) | collective-permute-done | bytes 327712 | tf_op jit(solution)/shard_map/ppermute | solution.py:464
  298.8 11.5 %collective-permute-done.21.refs_10_ = bf16[640,256]{1,0:T(8,128)(2,1)} collective-permute-done((bf16[640,256]{1,0:T(8,128)(2,1)}, bf16[640,256]{1,0:T(8,128)(2,1)}, u32[]{:S(2)}, u32[]{:S(2)}) %collective-permute-start.21) | collective-permute-done | bytes 327712 | tf_op jit(solution)/shard_map/ppermute | solution.py:464
  310.3 13.6 %shard_map.206 = (bf16[640,384]{1,0:T(8,128)(2,1)}, bf16[3,640,384]{2,1,0:T(8,128)(2,1)}, f32[2,128]{1,0:T(2,128)}) custom-call(s32[24]{0:T(128)} %concatenate.32.table, f32[3,640,384]{2,1,0:T(8,128)} %convolution_bitcast_fusion.proj, f32[2,128]{1,0:T(2,128)} %tile.10.gains, bf16[6,640,256]{2,1,0:T(8,128)(2,1)} %shard_map.204.local, ...), custom_call_target="tpu_custom_call" | custom-call | flops 1000000000 | bytes 10000000 | tf_op jit(solution)/shard_map/pallas_call | solution.py:404
  324.8 4.2 fusion.15
  343.9 85.5 %psum.37 = bf16[1,2816]{1,0:T(2,128)(2,1)S(1)} all-reduce(bf16[1,2816]{1,0:T(2,128)(2,1)S(1)} %pad_maximum_fusion.2), channel_id=1, replica_groups=mesh['seq'=16,'head'=2] {'seq'}, use_global_device_ids=true, to_apply=%region_12.13 | all-reduce | flops 2816 | bytes 11264 | tf_op jit(solution)/shard_map/psum | solution.py:518
  430.7 4.6 convert_element_type.120
  439.1 42.1 %all-reduce.5.cloned.1.call-done = (bf16[768,3,384]{2,0,1:T(8,128)(2,1)}, bf16[384,768]{1,0:T(8,128)(2,1)}) async-done(((bf16[768,3,384]{2,0,1:T(8,128)(2,1)}, bf16[384,768]{1,0:T(8,128)(2,1)}), (bf16[768,3,384]{2,0,1:T(8,128)(2,1)}, bf16[384,768]{1,0:T(8,128)(2,1)})) %all-reduce.5.cloned.1.call-update) | async-done | bytes 2359312 | tf_op jit(solution)/shard_map/psum | solution.py:518
  (158 shorter events, 76.3 us)
Async XLA Ops:
  7.2 329.3 %all-reduce.7.cloned.1.call-start = ((), (), s32[]{:S(2)}) async-start(), calls=%async_computation.1 | async-start | bytes 9437184 | tf_op jit(solution)/shard_map/psum | solution.py:496
  7.2 13.9 %collective-permute-start = (bf16[640,384]{1,0:T(8,128)(2,1)}, bf16[640,384]{1,0:T(8,128)(2,1)S(1)}, u32[]{:S(2)}, u32[]{:S(2)}) collective-permute-start(bf16[640,384]{1,0:T(8,128)(2,1)} %param.12), channel_id=1, source_target_pairs={{0,1},{1,0},{2,3},{3,2},{4,5},{5,4},{6,7},{7,6},{8,9},{9,8},{10,11... | collective-permute-start | bytes 1474568 | tf_op jit(solution)/shard_map/ppermute | solution.py:446
  7.8 14.1 %collective-permute-start.1 = (bf16[640,384]{1,0:T(8,128)(2,1)}, bf16[640,384]{1,0:T(8,128)(2,1)}, u32[]{:S(2)}, u32[]{:S(2)}) collective-permute-start(bf16[640,384]{1,0:T(8,128)(2,1)} %param.23), channel_id=1, source_target_pairs={{0,1},{1,0},{2,3},{3,2},{4,5},{5,4},{6,7},{7,6},{8,9},{9,8},{10,11... | collective-permute-start | bytes 1474568 | tf_op jit(solution)/shard_map/ppermute | solution.py:446
  38.9 42.3 %collective-permute-start.2 = (bf16[640,256]{1,0:T(8,128)(2,1)}, bf16[640,256]{1,0:T(8,128)(2,1)}, u32[]{:S(2)}, u32[]{:S(2)}) collective-permute-start(bf16[640,256]{1,0:T(8,128)(2,1)} %get-tuple-element.43), channel_id=1, source_target_pairs={{0,10},{2,12},{4,14},{6,16},{8,18},{10,20},{12,22},{14,24},{16,26}... | collective-permute-start | bytes 983048 | tf_op jit(solution)/shard_map/ppermute | solution.py:464
  45.4 37.1 %collective-permute-start.3 = (bf16[640,256]{1,0:T(8,128)(2,1)}, bf16[640,256]{1,0:T(8,128)(2,1)}, u32[]{:S(2)}, u32[]{:S(2)}) collective-permute-start(bf16[640,256]{1,0:T(8,128)(2,1)} %get-tuple-element.44), channel_id=1, source_target_pairs={{0,8},{2,10},{4,12},{6,14},{8,16},{10,18},{12,20},{14,22},{16,24},... | collective-permute-start | bytes 983048 | tf_op jit(solution)/shard_map/ppermute | solution.py:464
  49.6 34.2 %collective-permute-start.4 = (bf16[640,256]{1,0:T(8,128)(2,1)}, bf16[640,256]{1,0:T(8,128)(2,1)}, u32[]{:S(2)}, u32[]{:S(2)}) collective-permute-start(bf16[640,256]{1,0:T(8,128)(2,1)} %get-tuple-element.45), channel_id=1, source_target_pairs={{0,6},{2,8},{4,10},{6,12},{8,14},{10,16},{12,18},{14,20},{16,22},{... | collective-permute-start | bytes 983048 | tf_op jit(solution)/shard_map/ppermute | solution.py:464
  54.0 31.1 %collective-permute-start.5 = (bf16[640,256]{1,0:T(8,128)(2,1)}, bf16[640,256]{1,0:T(8,128)(2,1)}, u32[]{:S(2)}, u32[]{:S(2)}) collective-permute-start(bf16[640,256]{1,0:T(8,128)(2,1)} %get-tuple-element.46), channel_id=1, source_target_pairs={{0,4},{2,6},{4,8},{6,10},{8,12},{10,14},{12,16},{14,18},{16,20},{1... | collective-permute-start | bytes 983048 | tf_op jit(solution)/shard_map/ppermute | solution.py:464
  57.5 29.0 %collective-permute-start.6 = (bf16[640,256]{1,0:T(8,128)(2,1)}, bf16[640,256]{1,0:T(8,128)(2,1)}, u32[]{:S(2)}, u32[]{:S(2)}) collective-permute-start(bf16[640,256]{1,0:T(8,128)(2,1)} %get-tuple-element.47), channel_id=1, source_target_pairs={{0,2},{2,4},{4,6},{6,8},{8,10},{10,12},{12,14},{14,16},{16,18},{18... | collective-permute-start | bytes 983048 | tf_op jit(solution)/shard_map/ppermute | solution.py:464
  81.1 400.1 %all-reduce.5.cloned.1.call-start = ((), (), s32[]{:S(2)}) async-start(), calls=%async_computation | async-start | bytes 4718592 | tf_op jit(solution)/shard_map/psum | solution.py:518
  81.2 18.8 %collective-permute-start.7 = (bf16[640,256]{1,0:T(8,128)(2,1)}, bf16[640,256]{1,0:T(8,128)(2,1)S(1)}, u32[]{:S(2)}, u32[]{:S(2)}) collective-permute-start(bf16[640,256]{1,0:T(8,128)(2,1)} %get-tuple-element.49), channel_id=1, source_target_pairs={{2,0},{4,2},{6,4},{8,6},{10,8},{12,10},{14,12},{16,14},{18,16},{20... | collective-permute-start | bytes 983048 | tf_op jit(solution)/shard_map/ppermute | solution.py:464
  82.5 25.3 %collective-permute-start.8 = (bf16[640,256]{1,0:T(8,128)(2,1)}, bf16[640,256]{1,0:T(8,128)(2,1)}, u32[]{:S(2)}, u32[]{:S(2)}) collective-permute-start(bf16[640,256]{1,0:T(8,128)(2,1)} %get-tuple-element.50), channel_id=1, source_target_pairs={{4,0},{6,2},{8,4},{10,6},{12,8},{14,10},{16,12},{18,14},{20,16},{2... | collective-permute-start | bytes 983048 | tf_op jit(solution)/shard_map/ppermute | solution.py:464
  83.8 26.4 %collective-permute-start.9 = (bf16[640,256]{1,0:T(8,128)(2,1)}, bf16[640,256]{1,0:T(8,128)(2,1)}, u32[]{:S(2)}, u32[]{:S(2)}) collective-permute-start(bf16[640,256]{1,0:T(8,128)(2,1)} %get-tuple-element.51), channel_id=1, source_target_pairs={{6,0},{8,2},{10,4},{12,6},{14,8},{16,10},{18,12},{20,14},{22,16},{... | collective-permute-start | bytes 983048 | tf_op jit(solution)/shard_map/ppermute | solution.py:464
  85.1 64.2 %collective-permute-start.10 = (bf16[640,256]{1,0:T(8,128)(2,1)}, bf16[640,256]{1,0:T(8,128)(2,1)}, u32[]{:S(2)}, u32[]{:S(2)}) collective-permute-start(bf16[640,256]{1,0:T(8,128)(2,1)} %get-tuple-element.52), channel_id=1, source_target_pairs={{8,0},{10,2},{12,4},{14,6},{16,8},{18,10},{20,12},{22,14},{24,16},... | collective-permute-start | bytes 983048 | tf_op jit(solution)/shard_map/ppermute | solution.py:464
  86.4 65.4 %collective-permute-start.11 = (bf16[640,256]{1,0:T(8,128)(2,1)}, bf16[640,256]{1,0:T(8,128)(2,1)}, u32[]{:S(2)}, u32[]{:S(2)}) collective-permute-start(bf16[640,256]{1,0:T(8,128)(2,1)} %get-tuple-element.53), channel_id=1, source_target_pairs={{10,0},{12,2},{14,4},{16,6},{18,8},{20,10},{22,12},{24,14},{26,16}... | collective-permute-start | bytes 983048 | tf_op jit(solution)/shard_map/ppermute | solution.py:464
  199.5 50.6 %collective-permute-start.12 = (bf16[640,256]{1,0:T(8,128)(2,1)}, bf16[640,256]{1,0:T(8,128)(2,1)S(1)}, u32[]{:S(2)}, u32[]{:S(2)}) collective-permute-start(bf16[640,256]{1,0:T(8,128)(2,1)} %get-tuple-element.54), channel_id=1, source_target_pairs={{0,10},{2,12},{4,14},{6,16},{8,18},{10,20},{12,22},{14,24},{16,26}... | collective-permute-start | bytes 983048 | tf_op jit(solution)/shard_map/ppermute | solution.py:464
  202.5 48.9 %collective-permute-start.13 = (bf16[640,256]{1,0:T(8,128)(2,1)}, bf16[640,256]{1,0:T(8,128)(2,1)}, u32[]{:S(2)}, u32[]{:S(2)}) collective-permute-start(bf16[640,256]{1,0:T(8,128)(2,1)} %get-tuple-element.55), channel_id=1, source_target_pairs={{0,8},{2,10},{4,12},{6,14},{8,16},{10,18},{12,20},{14,22},{16,24},... | collective-permute-start | bytes 983048 | tf_op jit(solution)/shard_map/ppermute | solution.py:464
  211.2 41.5 %collective-permute-start.14 = (bf16[640,256]{1,0:T(8,128)(2,1)}, bf16[640,256]{1,0:T(8,128)(2,1)}, u32[]{:S(2)}, u32[]{:S(2)}) collective-permute-start(bf16[640,256]{1,0:T(8,128)(2,1)} %get-tuple-element.56), channel_id=1, source_target_pairs={{0,6},{2,8},{4,10},{6,12},{8,14},{10,16},{12,18},{14,20},{16,22},{... | collective-permute-start | bytes 983048 | tf_op jit(solution)/shard_map/ppermute | solution.py:464
  224.6 29.5 %collective-permute-start.15 = (bf16[640,256]{1,0:T(8,128)(2,1)}, bf16[640,256]{1,0:T(8,128)(2,1)}, u32[]{:S(2)}, u32[]{:S(2)}) collective-permute-start(bf16[640,256]{1,0:T(8,128)(2,1)} %get-tuple-element.57), channel_id=1, source_target_pairs={{0,4},{2,6},{4,8},{6,10},{8,12},{10,14},{12,16},{14,18},{16,20},{1... | collective-permute-start | bytes 983048 | tf_op jit(solution)/shard_map/ppermute | solution.py:464
  243.5 11.9 %collective-permute-start.16 = (bf16[640,256]{1,0:T(8,128)(2,1)}, bf16[640,256]{1,0:T(8,128)(2,1)}, u32[]{:S(2)}, u32[]{:S(2)}) collective-permute-start(bf16[640,256]{1,0:T(8,128)(2,1)} %get-tuple-element.58), channel_id=1, source_target_pairs={{0,2},{2,4},{4,6},{6,8},{8,10},{10,12},{12,14},{14,16},{16,18},{18... | collective-permute-start | bytes 983048 | tf_op jit(solution)/shard_map/ppermute | solution.py:464
  250.1 24.9 %collective-permute-start.17 = (bf16[640,256]{1,0:T(8,128)(2,1)}, bf16[640,256]{1,0:T(8,128)(2,1)}, u32[]{:S(2)}, u32[]{:S(2)}) collective-permute-start(bf16[640,256]{1,0:T(8,128)(2,1)} %get-tuple-element.60), channel_id=1, source_target_pairs={{2,0},{4,2},{6,4},{8,6},{10,8},{12,10},{14,12},{16,14},{18,16},{20... | collective-permute-start | bytes 983048 | tf_op jit(solution)/shard_map/ppermute | solution.py:464
  251.4 23.6 %collective-permute-start.18 = (bf16[640,256]{1,0:T(8,128)(2,1)}, bf16[640,256]{1,0:T(8,128)(2,1)}, u32[]{:S(2)}, u32[]{:S(2)}) collective-permute-start(bf16[640,256]{1,0:T(8,128)(2,1)} %get-tuple-element.61), channel_id=1, source_target_pairs={{4,0},{6,2},{8,4},{10,6},{12,8},{14,10},{16,12},{18,14},{20,16},{2... | collective-permute-start | bytes 983048 | tf_op jit(solution)/shard_map/ppermute | solution.py:464
  252.7 22.3 %collective-permute-start.19 = (bf16[640,256]{1,0:T(8,128)(2,1)}, bf16[640,256]{1,0:T(8,128)(2,1)}, u32[]{:S(2)}, u32[]{:S(2)}) collective-permute-start(bf16[640,256]{1,0:T(8,128)(2,1)} %get-tuple-element.62), channel_id=1, source_target_pairs={{6,0},{8,2},{10,4},{12,6},{14,8},{16,10},{18,12},{20,14},{22,16},{... | collective-permute-start | bytes 983048 | tf_op jit(solution)/shard_map/ppermute | solution.py:464
  254.1 44.7 %collective-permute-start.20 = (bf16[640,256]{1,0:T(8,128)(2,1)}, bf16[640,256]{1,0:T(8,128)(2,1)}, u32[]{:S(2)}, u32[]{:S(2)}) collective-permute-start(bf16[640,256]{1,0:T(8,128)(2,1)} %get-tuple-element.63), channel_id=1, source_target_pairs={{8,0},{10,2},{12,4},{14,6},{16,8},{18,10},{20,12},{22,14},{24,16},... | collective-permute-start | bytes 983048 | tf_op jit(solution)/shard_map/ppermute | solution.py:464
  255.4 54.9 %collective-permute-start.21 = (bf16[640,256]{1,0:T(8,128)(2,1)}, bf16[640,256]{1,0:T(8,128)(2,1)}, u32[]{:S(2)}, u32[]{:S(2)}) collective-permute-start(bf16[640,256]{1,0:T(8,128)(2,1)} %get-tuple-element.64), channel_id=1, source_target_pairs={{10,0},{12,2},{14,4},{16,6},{18,8},{20,10},{22,12},{24,14},{26,16}... | collective-permute-start | bytes 983048 | tf_op jit(solution)/shard_map/ppermute | solution.py:464
  (31 other events, 320.0 us)
Sparse Core Ops, SparseCore 0:
  81.3 248.2 all-reduce.6
  336.7 144.4 all-reduce.4

commit v2 on v1

--- a/solution.py
+++ b/solution.py
@@ -13,6 +13,7 @@
 F32 = jnp.float32
 BF16 = jnp.bfloat16
 TILE = 256
+GROUP = 4
 VMEM_LIMIT = 60 * 1024 * 1024
 
 
@@ -40,16 +41,12 @@
 
 
 def half_means(block):
-    left = lax.broadcasted_iota(jnp.int32, (128, 128), 0) // HS
-    right = lax.broadcasted_iota(jnp.int32, (128, 128), 1) // HS
-    averager = jnp.where(left == right, 1.0 / HS, 0.0).astype(F32)
-    return lax.dot_general(
-        block,
-        averager,
-        (((1,), (0,)), ((), ())),
-        precision=lax.Precision.HIGHEST,
-        preferred_element_type=F32,
-    )
+    left = (lax.broadcasted_iota(jnp.int32, (256, 128), 0) % 128) // HS
+    right = lax.broadcasted_iota(jnp.int32, (256, 128), 1) // HS
+    averager = jnp.where(left == right, 1.0 / HS, 0.0).astype(BF16)
+    coarse = block.astype(BF16)
+    fine = (block - coarse.astype(F32)).astype(BF16)
+    return dot_nn(jnp.concatenate([coarse, fine], axis=1), averager)
 
 
 def normalized_halves(block):
@@ -156,12 +153,15 @@
         lead = first - aligned
         tiles = (lead + length + TILE - 1) // TILE
         tiles = jnp.where(length > 0, tiles, 0)
+        groups = (tiles + GROUP - 1) // GROUP
+        grouped = (tiles > 2) & (tiles < max_tiles)
+        prepared = jnp.where(grouped, groups * GROUP, tiles)
 
         def inside(t):
             at = row + t * TILE
             return (at >= lead) & (at < lead + length)
 
-        @pl.loop(0, tiles)
+        @pl.loop(0, prepared)
         def _(t):
             at = pl.multiple_of(t * TILE, TILE)
             source = pl.ds(aligned + at, TILE)
@@ -208,7 +208,33 @@
                 d_query = dot_nn(eb[...], kb[...])
                 store(t, slice(0, 128), jnp.where(low, mixture, pltpu.roll(d_query, HS, 1)))
 
-        @pl.when((tiles > 0) & (tiles < max_tiles))
+        @pl.when(grouped)
+        def _():
+            @pl.loop(0, tiles)
+            def _(t):
+                at = pl.ds(pl.multiple_of(t * TILE, TILE), TILE)
+                q = qb[at, :]
+
+                def mix(g, total):
+                    for s in range(GROUP):
+                        first_pass(q, pl.ds(pl.multiple_of((g * GROUP + s) * TILE, TILE), TILE))
+                    to = pl.ds(pl.multiple_of(g * GROUP * TILE, GROUP * TILE), GROUP * TILE)
+                    return total + dot_nn(eb[:, to], vb[to, :])
+
+                mixed = lax.fori_loop(0, groups, mix, jnp.zeros((TILE, 128), F32))
+                mixture, scaled = softmax_tail(mixed, db[at, :].astype(F32))
+
+                def back(g, total):
+                    for s in range(GROUP):
+                        to = pl.ds(pl.multiple_of((g * GROUP + s) * TILE, TILE), TILE)
+                        second_pass(q, scaled, to)
+                    to = pl.ds(pl.multiple_of(g * GROUP * TILE, GROUP * TILE), GROUP * TILE)
+                    return total + dot_nn(eb[:, to], kb[to, :])
+
+                d_query = lax.fori_loop(0, groups, back, jnp.zeros((TILE, 128), F32))
+                store(t, slice(0, 128), jnp.where(low, mixture, pltpu.roll(d_query, HS, 1)))
+
+        @pl.when((tiles > 0) & (tiles <= 2))
         def _():
             @pl.loop(0, tiles)
             def _(t):
@@ -271,10 +297,10 @@
             out[h, :, 128:256] = jnp.concatenate([d_key, d_value], axis=0).T.astype(BF16)
 
 
-def unpack_kernel(heads, reach, table, proj, gains, local, *refs):
+def unpack_kernel(heads, reach, table, proj, gains, local, normed, cot, *refs):
     count = 2 * reach + 1
     backs = refs[:count]
-    attended, d_proj, gain_sums, stacked, sems = refs[count:]
+    attended, d_proj, gain_sums, grads, stacked, sems = refs[count:]
     rows = proj.shape[1]
 
     def copy_in(b):
@@ -320,6 +346,69 @@
         d_proj[1, :, lanes] = k_raw.astype(BF16)
         d_proj[2, :, lanes] = d_value.astype(BF16)
     gain_sums[...] = jnp.concatenate([q_sum * (HS**-0.5), k_sum], axis=0)
+    width, columns = normed.shape[1], heads * HS
+    for part in range(3):
+        grads[part * width : (part + 1) * width, :] = dot_tn(normed[...], d_proj[part]).astype(BF16)
+    for part in range(width // columns):
+        at = 3 * width + part * columns
+        lanes = slice(part * columns, (part + 1) * columns)
+        grads[at : at + columns, :] = dot_tn(attended[...], cot[:, lanes]).astype(BF16)
+
+
+class SeqSum:
+    def __init__(self, blocks, place, n_seq, small=None):
+        width = n_seq.bit_length() - 1
+        self.n_seq = n_seq
+        stages = [(bit, 1 << min(2, width - bit)) for bit in range(0, width, 2)]
+        self.order = stages + stages[::-1]
+        self.phases = len(self.order)
+        self.codes = {bit: (place >> bit) & (radix - 1) for bit, radix in stages}
+        self.current, self.small = blocks, small
+
+    def describe(self, phase):
+        bit, radix = self.order[phase]
+        adding = phase < self.phases // 2
+        joins = self.small is not None and adding == (bit > 0)
+        return bit, radix, adding, joins, self.codes[bit]
+
+    def split(self, radix):
+        rows, lanes = self.current.shape
+        return self.current.reshape(radix, rows // radix, lanes)
+
+    def send(self, phase):
+        bit, radix, adding, joins, code = self.describe(phase)
+        tail = self.small.astype(BF16) if joins else None
+        arrived = []
+        for mask in reversed(range(1, radix)):
+            block = self.current
+            if adding:
+                block = lax.dynamic_index_in_dim(self.split(radix), code ^ mask, 0, keepdims=False)
+            if joins:
+                block = jnp.concatenate([block, tail], axis=0)
+            route = [(i, i ^ (mask << bit)) for i in range(self.n_seq)]
+            arrived.append(lax.ppermute(block, "seq", route))
+        return arrived
+
+    def receive(self, phase, arrived):
+        bit, radix, adding, joins, code = self.describe(phase)
+        rows, lanes = self.current.shape
+        height = rows // radix if adding else rows
+        if adding:
+            total = lax.dynamic_index_in_dim(self.split(radix), code, 0, keepdims=False).astype(F32)
+            for block in arrived:
+                total = total + block[:height].astype(F32)
+            self.current = total.astype(BF16)
+        else:
+            whole = jnp.zeros((radix, height, lanes), BF16)
+            whole = lax.dynamic_update_index_in_dim(whole, self.current, code, 0)
+            for mask, block in zip(reversed(range(1, radix)), arrived):
+                whole = lax.dynamic_update_index_in_dim(whole, block[:height], code ^ mask, 0)
+            self.current = whole.reshape(radix * height, lanes)
+        if joins:
+            small = self.small.astype(BF16).astype(F32)
+            for block in arrived:
+                small = small + block[height:].astype(F32)
+            self.small = small
 
 
 def in_vmem():
@@ -361,7 +450,7 @@
 def work(reach, tok_rows, table, blocks):
     count = 2 * reach + 1
     max_tiles = -(-(LONG_LEN + 15) // TILE)
-    padded = count * tok_rows + TILE
+    padded = count * tok_rows + GROUP * TILE
     span = max_tiles * TILE
     return pl.pallas_call(
         functools.partial(work_kernel, reach, tok_rows, max_tiles),
@@ -397,7 +486,7 @@
     )(table, local, ids_row, ids_column)
 
 
-def unpack(heads, reach, table, proj, gains, local, backs):
+def unpack(heads, reach, table, proj, gains, local, normed, cot, backs):
     rows = proj.shape[1]
     count = 2 * reach + 1
     width = heads * HS
@@ -407,16 +496,17 @@
             jax.ShapeDtypeStruct((rows, width), BF16),
             jax.ShapeDtypeStruct((3, rows, width), BF16),
             jax.ShapeDtypeStruct((2, 128), F32),
+            jax.ShapeDtypeStruct((4 * normed.shape[1], width), BF16),
         ],
-        in_specs=[in_smem(), in_vmem(), in_vmem(), in_vmem()] + [anywhere()] * count,
-        out_specs=[in_vmem()] * 3,
+        in_specs=[in_smem()] + [in_vmem()] * 5 + [anywhere()] * count,
+        out_specs=[in_vmem()] * 4,
         scratch_shapes=[
             pltpu.VMEM((count, rows, 4 * HS), BF16),
             pltpu.SemaphoreType.DMA((count,)),
         ],
         compiler_params=compiler_params(),
         cost_estimate=cost(10**9, 10**7),
-    )(table, proj, gains, local, *backs)
+    )(table, proj, gains, local, normed, cot, *backs)
 
 
 def on_device(
@@ -441,6 +531,7 @@
     place = lax.axis_index("seq")
     side = lax.axis_index("head")
     assert heads == reach + 1 and n_seq >= heads and heads % 2 == 0
+    assert n_seq & (n_seq - 1) == 0 and half == local_width
 
     def from_peer(block):
         return lax.ppermute(block, "head", [(0, 1), (1, 0)])
@@ -479,65 +570,81 @@
     proj = jnp.einsum("td,dkc->ktc", normed, w_qkv, preferred_element_type=F32)
     d_attended = jnp.einsum("td,cd->tc", cot_whole, w_attn_out, preferred_element_type=F32)
     packed = pack(heads, reach, table, proj, d_attended.astype(BF16), gains)
+    packed, normed_ff, cot_ff = lax.optimization_barrier((packed, normed, cot_whole))
     slots, local = packed[:-1], packed[-1]
 
     arrived = [shifted(slots[reach + d], d) for d in range(reach, -reach - 1, -1)]
 
-    up_input = jnp.dot(normed, w_up, preferred_element_type=F32) + up_bias
+    up_input = jnp.dot(normed_ff, w_up, preferred_element_type=F32) + up_bias
     hidden_f, gelu_pull = jax.vjp(exact_gelu, up_input)
     hidden = hidden_f.astype(BF16)
-    d_hidden = jnp.einsum("td,fd->tf", cot_whole, w_down, preferred_element_type=F32)
+    d_hidden = jnp.einsum("td,fd->tf", cot_ff, w_down, preferred_element_type=F32)
     d_upper_f = gelu_pull(d_hidden)[0]
     d_upper = d_upper_f.astype(BF16)
-    grad_down = jnp.einsum("tf,td->fd", hidden, cot_whole, preferred_element_type=F32)
-    grad_up = jnp.einsum("td,tf->df", normed, d_upper, preferred_element_type=F32)
+    grad_down = jnp.einsum("tf,td->fd", hidden, cot_ff, preferred_element_type=F32)
+    grad_up = jnp.einsum("td,tf->df", normed_ff, d_upper, preferred_element_type=F32)
     grad_out_bias = jnp.sum(cotangent.astype(F32), axis=0)
     grad_up_bias = jnp.sum(d_upper.astype(F32), axis=0)
-    early = lax.psum((grad_down.astype(BF16), grad_up.astype(BF16)), "seq")
+    early = (grad_down.astype(BF16), grad_up.astype(BF16))
+    early, arrived = lax.optimization_barrier((early, arrived))
+    early = lax.psum(early, "seq")
     ffn_out = jnp.dot(hidden, w_down, preferred_element_type=F32)
     ffn_back = jnp.einsum("tf,df->td", d_upper, w_up, preferred_element_type=F32)
 
     local_out = local_work(heads, table, local, ids_row, ids_column)
     worked = work(reach, tok_rows, table, arrived)
     returned = [shifted(worked[b], b - reach) for b in range(2 * reach + 1)][::-1]
-    attended, d_proj, gain_sums = unpack(heads, reach, table, proj, gains, local_out, returned)
+    attended, d_proj, gain_sums, late = unpack(
+        heads, reach, table, proj, gains, local_out, normed, cot_whole, returned
+    )
 
     partial_out = jnp.dot(attended, w_attn_out, preferred_element_type=F32) + ffn_out
     summed = add_over_heads(partial_out)
     block_out = (summed + tokens.astype(F32) + out_bias).astype(BF16)
-    grad_attn_out = jnp.einsum("tc,td->cd", attended, cot_whole, preferred_element_type=F32)
-    grad_qkv = jnp.einsum("td,ktc->dkc", normed, d_proj, preferred_element_type=F32)
     d_normed = ffn_back + jnp.einsum("ktc,dkc->td", d_proj, w_qkv, preferred_element_type=F32)
     d_input, d_ln = norm_pull(d_normed)
     input_sum = add_over_heads(d_input)
     tokens_grad = (input_sum + cotangent.astype(F32)).astype(BF16)
+
+    half_gain = HS // 2
     gain_total = gain_sums[:, :HS] + gain_sums[:, HS:]
-    small = jnp.concatenate([d_ln, gain_total.reshape(-1), grad_up_bias, grad_out_bias])
-    parts = (grad_qkv.astype(BF16), grad_attn_out.astype(BF16), small[None].astype(BF16))
-    parts, early = lax.optimization_barrier((parts, early))
-    late = lax.psum(parts, "seq")
-    sums = late[2][0].astype(F32)
+    by_side = [
+        jnp.concatenate([d_ln[i * half : (i + 1) * half], gain_total[:, i * half_gain : (i + 1) * half_gain].reshape(-1)])
+        for i in range(2)
+    ]
+    own = jnp.where(side == 0, by_side[0], by_side[1])
+    norms = own + from_peer(jnp.where(side == 0, by_side[1], by_side[0]))
+    small = jnp.concatenate([norms, grad_up_bias, grad_out_bias])
+    small_size = small.shape[0]
+    small_rows = -(-small_size // (16 * half)) * 16
+    small = jnp.pad(small, (0, small_rows * half - small_size)).reshape(small_rows, half)
+    late = SeqSum(late, place, n_seq, small)
+    for phase in range(late.phases):
+        coming = late.send(phase)
+        if phase == 0:
+            coming, early = lax.optimization_barrier((coming, early))
+        late.receive(phase, coming)
+    small = late.small
+    sums = late.current.astype(F32)
     width = 2 * half
-    shared = add_over_heads(sums[None, :width])[0]
-    gain_pair = sums[width : width + 2 * HS].reshape(2, HS)
-    gain_half = HS // 2
-    gain_send = jnp.where(side == 0, gain_pair[:, gain_half:], gain_pair[:, :gain_half])
-    gain_keep = jnp.where(side == 0, gain_pair[:, :gain_half], gain_pair[:, gain_half:])
-    gain_grads = gain_keep + from_peer(gain_send)
-    at = width + 2 * HS
-    up_width = up_bias.shape[0]
+    qkv_rows = 3 * width
+    qkv_sum = sums[:qkv_rows].reshape(3, width, local_width).transpose(1, 0, 2)
+    out_sum = jnp.concatenate(jnp.split(sums[qkv_rows:], 2, 0), axis=1)
+    small = small.reshape(-1)
+    at_up = half + HS
+    at_out = at_up + up_bias.shape[0]
     return (
         block_out,
         tokens_grad,
-        shared,
-        late[0].astype(F32),
-        gain_grads[0],
-        gain_grads[1],
+        small[:half],
+        qkv_sum,
+        small[half : half + half_gain],
+        small[half + half_gain : at_up],
         early[1].astype(F32),
-        sums[at : at + up_width],
-        late[1].astype(F32),
+        small[at_up:at_out],
+        out_sum,
         early[0].astype(F32),
-        sums[at + up_width :],
+        small[at_out : at_out + half],
     )
 
 

time: 495 us -> 445 us (0.90); the launches traced: 493 us -> 437 us
  blocking collectives: 85.5 us -> 0 us
  starting transfers between devices: 82.4 us -> 108 us
  local copies, waits for them, and re-layouts: 8.89 us -> 21.3 us
  matrix products: 46.4 us -> 39.3 us
  Pallas kernels: 88.4 us -> 94.5 us
  waiting for transfers between devices: 136 us -> 130 us
    psum x1 -> x0, blocking collectives: 85.5 us -> none  [on_device(): late = lax.psum(parts, 'seq')]
    ppermute x0 -> x12, waiting for transfers between devices: none -> 70.7 us  [send(): arrived.append(lax.ppermute(block, 'seq', route))]
    ppermute x20, waiting for transfers between devices: 94.3 us -> 44 us  [shifted(): return lax.ppermute(block, 'seq', route)]
    psum x2 -> x1, waiting for transfers between devices: 42.1 us -> 15.5 us  [on_device(): early = lax.psum(early, 'seq')]
    ppermute x0 -> x12, starting transfers between devices: none -> 20.4 us  [send(): arrived.append(lax.ppermute(block, 'seq', route))]
    pallas_call x1, Pallas kernels: 18.2 us -> 28 us  [local_work(): pl.pallas_call(functools.partial(local_kernel, heads), out_shape=jax.Shap...]
    ppermute x20, starting transfers between devices: 80.5 us -> 86.3 us  [shifted(): return lax.ppermute(block, 'seq', route)]
    dot_general x6 -> x4, matrix products: 25.4 us -> 21.4 us  [the longest x1 10.8 us: on_device(): jnp.einsum('td,fd->tf', cot_ff, w_down, preferred_element_type=F32)]
  transfers between devices with their start and end apart: 28 -> 38, of which waited for: 9 -> 16; matrix products, arithmetic and copies ran while one was open for 13% -> 10% of each run, Pallas kernels for 16% -> 20%
where the time goes in v2:
time: 445 us; the launch traced here: 437 us
  waiting for transfers between devices  130 us (29%)
  starting transfers between devices  108 us (24%)
  Pallas kernels  94.5 us (21%)
  matrix products  39.3 us (9%)
  other arithmetic  25 us (6%)
  local copies, waits for them, and re-layouts  21.3 us (5%)
  between operations  19.7 us (4%)
    ppermute x20, starting transfers between devices, shifted(): return lax.ppermute(block, 'seq', route)  86.3 us
    ppermute x12, waiting for transfers between devices, send(): arrived.append(lax.ppermute(block, 'seq', route))  70.7 us
    pallas_call x1, Pallas kernels, work(): pl.pallas_call(functools.partial(work_kernel, reach, tok_rows, max_tiles)...  47.7 us
    ppermute x20, waiting for transfers between devices, shifted(): return lax.ppermute(block, 'seq', route)  44 us
    pallas_call x1, Pallas kernels, local_work(): pl.pallas_call(functools.partial(local_kernel, heads), out_shape=jax.Shap...  28 us
    ppermute x12, starting transfers between devices, send(): arrived.append(lax.ppermute(block, 'seq', route))  20.4 us
    psum x1, waiting for transfers between devices, on_device(): early = lax.psum(early, 'seq')  15.5 us
    pallas_call x1, Pallas kernels, unpack(): pl.pallas_call(functools.partial(unpack_kernel, heads, reach), out_shape=...  12.1 us
  transfers between devices with their start and end apart: 38, of which 16 were waited for; matrix products, arithmetic and copies ran while one was open for 10% of the time, Pallas kernels for 20%

profile of v2, /device:TPU:0, one launch (start us, length us, event | category | flops | bytes accessed | tf_op | source)
XLA Modules:
  0.0 437.5 jit_solution(12832515072180545929)
XLA Ops:
  31.4 6.7 %shard_map.203 = (bf16[640,256]{1,0:T(8,128)(2,1)}, bf16[640,256]{1,0:T(8,128)(2,1)}, bf16[640,256]{1,0:T(8,128)(2,1)}, bf16[640,256]{1,0:T(8,128)(2,1)}, bf16[6...) custom-call(s32[24]{0:T(128)} %concatenate.40.table, ...), custom_call_target="tpu_custom_call" | custom-call | flops 1000000000 | bytes 10000000 | tf_op jit(solution)/shard_map/pallas_call | solution.py:440
  41.9 10.8 %fusion.33 = (bf16[1536]{0:T(1024)(128)(2,1)S(1)}, bf16[640,1536]{1,0:T(8,128)(2,1)S(1)}, f32[640,1536]{1,0:T(8,128)S(1)}) fusion(f32[640,1536]{1,0:T(8,128)S(1)} %fusion.40, f32[1536]{0:T(1024)S(1)} %copy-done.28, bf16[640,768]{1,0:T(8,128)(2,1)S(1)} %copy-done.5, bf16[1536,768]{1,0:T(8,128)(2,1)S(1)} %copy-done), kind=kOutput, calls=%fused_computation.115 | convolution fusion | flops 1582692864 | bytes 13181952 | tf_op jit(solution)/shard_map/td,fd->tf/dot_general | solution.py:581
  56.8 6.0 %collective-permute-start.2 = (bf16[640,256]{1,0:T(8,128)(2,1)S(1)}, bf16[640,256]{1,0:T(8,128)(2,1)S(1)}, u32[]{:S(2)}, u32[]{:S(2)}) collective-permute-start(bf16[640,256]{1,0:T(8,128)(2,1)S(1)} %copy-done.42), channel_id=1, source_target_pairs={{0,10},{2,12},{4,14},{6,16},{8,18},{10,20},{12,22},{14,24},{16,26}... | collective-permute-start | bytes 983048 | tf_op jit(solution)/shard_map/ppermute | solution.py:555
  66.3 4.6 %collective-permute-start.4 = (bf16[640,256]{1,0:T(8,128)(2,1)S(1)}, bf16[640,256]{1,0:T(8,128)(2,1)S(1)}, u32[]{:S(2)}, u32[]{:S(2)}) collective-permute-start(bf16[640,256]{1,0:T(8,128)(2,1)S(1)} %copy-done.40), channel_id=1, source_target_pairs={{0,6},{2,8},{4,10},{6,12},{8,14},{10,16},{12,18},{14,20},{16,22},{... | collective-permute-start | bytes 983048 | tf_op jit(solution)/shard_map/ppermute | solution.py:555
  93.9 6.6 %collective-permute-done.8.refs_7_ = bf16[640,256]{1,0:T(8,128)(2,1)} collective-permute-done((bf16[640,256]{1,0:T(8,128)(2,1)}, bf16[640,256]{1,0:T(8,128)(2,1)}, u32[]{:S(2)}, u32[]{:S(2)}) %collective-permute-start.8) | collective-permute-done | bytes 327712 | tf_op jit(solution)/shard_map/ppermute | solution.py:555
  100.4 14.9 %collective-permute-done.10.refs_9_ = bf16[640,256]{1,0:T(8,128)(2,1)} collective-permute-done((bf16[640,256]{1,0:T(8,128)(2,1)}, bf16[640,256]{1,0:T(8,128)(2,1)}, u32[]{:S(2)}, u32[]{:S(2)}) %collective-permute-start.10) | collective-permute-done | bytes 327712 | tf_op jit(solution)/shard_map/ppermute | solution.py:555
  115.4 6.9 %collective-permute-done.11.refs_10_ = bf16[640,256]{1,0:T(8,128)(2,1)} collective-permute-done((bf16[640,256]{1,0:T(8,128)(2,1)S(1)}, bf16[640,256]{1,0:T(8,128)(2,1)}, u32[]{:S(2)}, u32[]{:S(2)}) %collective-permute-start.11) | collective-permute-done | bytes 327712 | tf_op jit(solution)/shard_map/ppermute | solution.py:555
  122.2 47.7 %shard_map.205 = (bf16[640,256]{1,0:T(8,128)(2,1)}, bf16[640,256]{1,0:T(8,128)(2,1)}, bf16[640,256]{1,0:T(8,128)(2,1)}, bf16[640,256]{1,0:T(8,128)(2,1)}, bf16[6...) custom-call(s32[24]{0:T(128)} %concatenate.40.table, ...), custom_call_target="tpu_custom_call" | custom-call | flops 30000001024 | bytes 10000000 | tf_op jit(solution)/shard_map/pallas_call | solution.py:455
  169.9 44.9 %collective-permute-start.12 = (bf16[640,256]{1,0:T(8,128)(2,1)}, bf16[640,256]{1,0:T(8,128)(2,1)S(1)}, u32[]{:S(2)}, u32[]{:S(2)}) collective-permute-start(bf16[640,256]{1,0:T(8,128)(2,1)} %get-tuple-element.107), channel_id=1, source_target_pairs={{0,10},{2,12},{4,14},{6,16},{8,18},{10,20},{12,22},{14,24},{16,26}... | collective-permute-start | bytes 983048 | tf_op jit(solution)/shard_map/ppermute | solution.py:555
  217.5 4.6 %collective-permute-start.15 = (bf16[640,256]{1,0:T(8,128)(2,1)}, bf16[640,256]{1,0:T(8,128)(2,1)S(1)}, u32[]{:S(2)}, u32[]{:S(2)}) collective-permute-start(bf16[640,256]{1,0:T(8,128)(2,1)} %get-tuple-element.110), channel_id=1, source_target_pairs={{0,4},{2,6},{4,8},{6,10},{8,12},{10,14},{12,16},{14,18},{16,20},{1... | collective-permute-start | bytes 983048 | tf_op jit(solution)/shard_map/ppermute | solution.py:555
  223.4 5.4 %fusion.42 = f32[640,768]{1,0:T(8,128)} fusion(bf16[640,1536]{1,0:T(8,128)(2,1)} %copy-done.43, bf16[768,1536]{1,0:T(8,128)(2,1)} %param.18), kind=kOutput, calls=%fused_computation.123 | convolution fusion | flops 1509949440 | bytes 6291456 | tf_op jit(solution)/shard_map/tf,df->td/dot_general | solution.py:592
  241.7 28.0 %shard_map.204.local = bf16[6,640,256]{2,1,0:T(8,128)(2,1)} custom-call(s32[24]{0:T(128)} %concatenate.40.table, bf16[6,640,256]{2,1,0:T(8,128)(2,1)} %get-tuple-element.82.local, s32[1,640]{1,0:T(1,128)} %and_select_fusion.ids_row, s32[640,1]{1,0:T(8,128)} %reshape_select_fusion.ids_column), custom_call_target="tpu_custom_call" | custom-call | flops 5000000000 | bytes 4000000 | tf_op jit(solution)/shard_map/pallas_call | solution.py:479
  269.8 5.8 %collective-permute-done.21.refs_10_ = bf16[640,256]{1,0:T(8,128)(2,1)} collective-permute-done((bf16[640,256]{1,0:T(8,128)(2,1)}, bf16[640,256]{1,0:T(8,128)(2,1)}, u32[]{:S(2)}, u32[]{:S(2)}) %collective-permute-start.21) | collective-permute-done | bytes 327712 | tf_op jit(solution)/shard_map/ppermute | solution.py:555
  275.6 12.1 %shard_map.206 = (bf16[640,384]{1,0:T(8,128)(2,1)}, bf16[3,640,384]{2,1,0:T(8,128)(2,1)}, f32[2,128]{1,0:T(2,128)}, bf16[3072,384]{1,0:T(8,128)(2,1)}) custom-call(s32[24]{0:T(128)} %concatenate.40.table, f32[3,640,384]{2,1,0:T(8,128)} %convolution_bitcast_fusion.proj, f32[2,128]{1,0:T(2,128)} %tile.10.gains, bf16[6,640,256]{2,1,0:T(8,128)(2,1)} %shard_map.204.local, ...), custom_call_target="tpu_custom_call" | custom-call | flops 1000000000 | bytes 10000000 | tf_op jit(solution)/shard_map/pallas_call | solution.py:493
  287.8 4.2 fusion.15
  299.2 7.4 %collective-permute-start.25 = (bf16[768,384]{1,0:T(8,128)(2,1)}, bf16[768,384]{1,0:T(8,128)(2,1)}, u32[]{:S(2)}, u32[]{:S(2)}) collective-permute-start(bf16[768,384]{1,0:T(8,128)(2,1)} %get-tuple-element.150), channel_id=1, source_target_pairs={{0,6},{2,4},{4,2},{6,0},{8,14},{10,12},{12,10},{14,8},{16,22},{18,... | collective-permute-start | bytes 1769480 | tf_op jit(solution)/shard_map/ppermute | solution.py:389
  309.2 22.7 %collective-permute-done.25 = bf16[768,384]{1,0:T(8,128)(2,1)} collective-permute-done((bf16[768,384]{1,0:T(8,128)(2,1)}, bf16[768,384]{1,0:T(8,128)(2,1)}, u32[]{:S(2)}, u32[]{:S(2)}) %collective-permute-start.25) | collective-permute-done | bytes 589856 | tf_op jit(solution)/shard_map/ppermute | solution.py:389
  331.9 11.9 %collective-permute-done.26 = bf16[768,384]{1,0:T(8,128)(2,1)} collective-permute-done((bf16[768,384]{1,0:T(8,128)(2,1)}, bf16[768,384]{1,0:T(8,128)(2,1)}, u32[]{:S(2)}, u32[]{:S(2)}) %collective-permute-start.26) | collective-permute-done | bytes 589856 | tf_op jit(solution)/shard_map/ppermute | solution.py:389
  343.8 15.5 %all-reduce.4.cloned.1.call-done = (bf16[1536,768]{1,0:T(8,128)(2,1)}, bf16[768,1536]{1,0:T(8,128)(2,1)}) async-done(((bf16[1536,768]{1,0:T(8,128)(2,1)}, bf16[768,1536]{1,0:T(8,128)(2,1)}), (bf16[1536,768]{1,0:T(8,128)(2,1)}, bf16[768,1536]{1,0:T(8,128)(2,1)})) %all-reduce.4.cloned.1.call-update) | async-done | bytes 4718608 | tf_op jit(solution)/shard_map/psum | solution.py:590
  369.4 7.0 %collective-permute-done.29 = bf16[208,384]{1,0:T(8,128)(2,1)S(1)} collective-permute-done((bf16[208,384]{1,0:T(8,128)(2,1)S(1)}, bf16[208,384]{1,0:T(8,128)(2,1)S(1)}, u32[]{:S(2)}, u32[]{:S(2)}) %collective-permute-start.29) | collective-permute-done | bytes 159776 | tf_op jit(solution)/shard_map/ppermute | solution.py:389
  381.1 4.2 collective-permute-done.31
  385.3 6.4 %collective-permute-done.32 = bf16[192,384]{1,0:T(8,128)(2,1)S(1)} collective-permute-done((bf16[192,384]{1,0:T(8,128)(2,1)S(1)}, bf16[192,384]{1,0:T(8,128)(2,1)S(1)}, u32[]{:S(2)}, u32[]{:S(2)}) %collective-permute-start.32) | collective-permute-done | bytes 147488 | tf_op jit(solution)/shard_map/ppermute | solution.py:389
  404.3 4.1 collective-permute-done.36
  408.4 11.1 %collective-permute-done.35 = bf16[784,384]{1,0:T(8,128)(2,1)S(1)} collective-permute-done((bf16[784,384]{1,0:T(8,128)(2,1)S(1)}, bf16[784,384]{1,0:T(8,128)(2,1)S(1)}, u32[]{:S(2)}, u32[]{:S(2)}) %collective-permute-start.35) | collective-permute-done | bytes 602144 | tf_op jit(solution)/shard_map/ppermute | solution.py:389
  (232 shorter events, 118.5 us)
Async XLA Ops:
  7.2 352.0 %all-reduce.4.cloned.1.call-start = ((), (), s32[]{:S(2)}) async-start(), calls=%async_computation | async-start | bytes 9437184 | tf_op jit(solution)/shard_map/psum | solution.py:590
  56.8 23.5 %collective-permute-start.2 = (bf16[640,256]{1,0:T(8,128)(2,1)S(1)}, bf16[640,256]{1,0:T(8,128)(2,1)S(1)}, u32[]{:S(2)}, u32[]{:S(2)}) collective-permute-start(bf16[640,256]{1,0:T(8,128)(2,1)S(1)} %copy-done.42), channel_id=1, source_target_pairs={{0,10},{2,12},{4,14},{6,16},{8,18},{10,20},{12,22},{14,24},{16,26}... | collective-permute-start | bytes 983048 | tf_op jit(solution)/shard_map/ppermute | solution.py:555
  62.8 18.9 %collective-permute-start.3 = (bf16[640,256]{1,0:T(8,128)(2,1)S(1)}, bf16[640,256]{1,0:T(8,128)(2,1)S(1)}, u32[]{:S(2)}, u32[]{:S(2)}) collective-permute-start(bf16[640,256]{1,0:T(8,128)(2,1)S(1)} %copy-done.41), channel_id=1, source_target_pairs={{0,8},{2,10},{4,12},{6,14},{8,16},{10,18},{12,20},{14,22},{16,24},... | collective-permute-start | bytes 983048 | tf_op jit(solution)/shard_map/ppermute | solution.py:555
  81.7 18.7 %collective-permute-start.8 = (bf16[640,256]{1,0:T(8,128)(2,1)}, bf16[640,256]{1,0:T(8,128)(2,1)}, u32[]{:S(2)}, u32[]{:S(2)}) collective-permute-start(bf16[640,256]{1,0:T(8,128)(2,1)} %get-tuple-element.92), channel_id=1, source_target_pairs={{4,0},{6,2},{8,4},{10,6},{12,8},{14,10},{16,12},{18,14},{20,16},{2... | collective-permute-start | bytes 983048 | tf_op jit(solution)/shard_map/ppermute | solution.py:555
  83.0 17.4 %collective-permute-start.9 = (bf16[640,256]{1,0:T(8,128)(2,1)}, bf16[640,256]{1,0:T(8,128)(2,1)}, u32[]{:S(2)}, u32[]{:S(2)}) collective-permute-start(bf16[640,256]{1,0:T(8,128)(2,1)} %get-tuple-element.93), channel_id=1, source_target_pairs={{6,0},{8,2},{10,4},{12,6},{14,8},{16,10},{18,12},{20,14},{22,16},{... | collective-permute-start | bytes 983048 | tf_op jit(solution)/shard_map/ppermute | solution.py:555
  87.8 27.6 %collective-permute-start.10 = (bf16[640,256]{1,0:T(8,128)(2,1)}, bf16[640,256]{1,0:T(8,128)(2,1)}, u32[]{:S(2)}, u32[]{:S(2)}) collective-permute-start(bf16[640,256]{1,0:T(8,128)(2,1)} %get-tuple-element.94), channel_id=1, source_target_pairs={{8,0},{10,2},{12,4},{14,6},{16,8},{18,10},{20,12},{22,14},{24,16},... | collective-permute-start | bytes 983048 | tf_op jit(solution)/shard_map/ppermute | solution.py:555
  89.1 33.1 %collective-permute-start.11 = (bf16[640,256]{1,0:T(8,128)(2,1)S(1)}, bf16[640,256]{1,0:T(8,128)(2,1)}, u32[]{:S(2)}, u32[]{:S(2)}) collective-permute-start(bf16[640,256]{1,0:T(8,128)(2,1)S(1)} %copy-done.35), channel_id=1, source_target_pairs={{10,0},{12,2},{14,4},{16,6},{18,8},{20,10},{22,12},{24,14},{26,16}... | collective-permute-start | bytes 983048 | tf_op jit(solution)/shard_map/ppermute | solution.py:555
  169.9 58.9 %collective-permute-start.12 = (bf16[640,256]{1,0:T(8,128)(2,1)}, bf16[640,256]{1,0:T(8,128)(2,1)S(1)}, u32[]{:S(2)}, u32[]{:S(2)}) collective-permute-start(bf16[640,256]{1,0:T(8,128)(2,1)} %get-tuple-element.107), channel_id=1, source_target_pairs={{0,10},{2,12},{4,14},{6,16},{8,18},{10,20},{12,22},{14,24},{16,26}... | collective-permute-start | bytes 983048 | tf_op jit(solution)/shard_map/ppermute | solution.py:555
  214.9 19.2 %collective-permute-start.13 = (bf16[640,256]{1,0:T(8,128)(2,1)}, bf16[640,256]{1,0:T(8,128)(2,1)S(1)}, u32[]{:S(2)}, u32[]{:S(2)}) collective-permute-start(bf16[640,256]{1,0:T(8,128)(2,1)} %get-tuple-element.108), channel_id=1, source_target_pairs={{0,8},{2,10},{4,12},{6,14},{8,16},{10,18},{12,20},{14,22},{16,24},... | collective-permute-start | bytes 983048 | tf_op jit(solution)/shard_map/ppermute | solution.py:555
  216.2 19.1 %collective-permute-start.14 = (bf16[640,256]{1,0:T(8,128)(2,1)}, bf16[640,256]{1,0:T(8,128)(2,1)S(1)}, u32[]{:S(2)}, u32[]{:S(2)}) collective-permute-start(bf16[640,256]{1,0:T(8,128)(2,1)} %get-tuple-element.109), channel_id=1, source_target_pairs={{0,6},{2,8},{4,10},{6,12},{8,14},{10,16},{12,18},{14,20},{16,22},{... | collective-permute-start | bytes 983048 | tf_op jit(solution)/shard_map/ppermute | solution.py:555
  217.5 21.6 %collective-permute-start.15 = (bf16[640,256]{1,0:T(8,128)(2,1)}, bf16[640,256]{1,0:T(8,128)(2,1)S(1)}, u32[]{:S(2)}, u32[]{:S(2)}) collective-permute-start(bf16[640,256]{1,0:T(8,128)(2,1)} %get-tuple-element.110), channel_id=1, source_target_pairs={{0,4},{2,6},{4,8},{6,10},{8,12},{10,14},{12,16},{14,18},{16,20},{1... | collective-permute-start | bytes 983048 | tf_op jit(solution)/shard_map/ppermute | solution.py:555
  222.1 18.3 %collective-permute-start.16 = (bf16[640,256]{1,0:T(8,128)(2,1)}, bf16[640,256]{1,0:T(8,128)(2,1)S(1)}, u32[]{:S(2)}, u32[]{:S(2)}) collective-permute-start(bf16[640,256]{1,0:T(8,128)(2,1)} %get-tuple-element.111), channel_id=1, source_target_pairs={{0,2},{2,4},{4,6},{6,8},{8,10},{10,12},{12,14},{14,16},{16,18},{18... | collective-permute-start | bytes 983048 | tf_op jit(solution)/shard_map/ppermute | solution.py:555
  228.8 40.9 %collective-permute-start.17 = (bf16[640,256]{1,0:T(8,128)(2,1)}, bf16[640,256]{1,0:T(8,128)(2,1)S(1)}, u32[]{:S(2)}, u32[]{:S(2)}) collective-permute-start(bf16[640,256]{1,0:T(8,128)(2,1)} %get-tuple-element.113), channel_id=1, source_target_pairs={{2,0},{4,2},{6,4},{8,6},{10,8},{12,10},{14,12},{16,14},{18,16},{20... | collective-permute-start | bytes 983048 | tf_op jit(solution)/shard_map/ppermute | solution.py:555
  234.1 35.7 %collective-permute-start.18 = (bf16[640,256]{1,0:T(8,128)(2,1)}, bf16[640,256]{1,0:T(8,128)(2,1)S(1)}, u32[]{:S(2)}, u32[]{:S(2)}) collective-permute-start(bf16[640,256]{1,0:T(8,128)(2,1)} %get-tuple-element.114), channel_id=1, source_target_pairs={{4,0},{6,2},{8,4},{10,6},{12,8},{14,10},{16,12},{18,14},{20,16},{2... | collective-permute-start | bytes 983048 | tf_op jit(solution)/shard_map/ppermute | solution.py:555
  235.4 34.5 %collective-permute-start.19 = (bf16[640,256]{1,0:T(8,128)(2,1)}, bf16[640,256]{1,0:T(8,128)(2,1)S(1)}, u32[]{:S(2)}, u32[]{:S(2)}) collective-permute-start(bf16[640,256]{1,0:T(8,128)(2,1)} %get-tuple-element.115), channel_id=1, source_target_pairs={{6,0},{8,2},{10,4},{12,6},{14,8},{16,10},{18,12},{20,14},{22,16},{... | collective-permute-start | bytes 983048 | tf_op jit(solution)/shard_map/ppermute | solution.py:555
  239.1 30.7 %collective-permute-start.20 = (bf16[640,256]{1,0:T(8,128)(2,1)}, bf16[640,256]{1,0:T(8,128)(2,1)}, u32[]{:S(2)}, u32[]{:S(2)}) collective-permute-start(bf16[640,256]{1,0:T(8,128)(2,1)} %get-tuple-element.116), channel_id=1, source_target_pairs={{8,0},{10,2},{12,4},{14,6},{16,8},{18,10},{20,12},{22,14},{24,16},... | collective-permute-start | bytes 983048 | tf_op jit(solution)/shard_map/ppermute | solution.py:555
  240.4 35.2 %collective-permute-start.21 = (bf16[640,256]{1,0:T(8,128)(2,1)}, bf16[640,256]{1,0:T(8,128)(2,1)}, u32[]{:S(2)}, u32[]{:S(2)}) collective-permute-start(bf16[640,256]{1,0:T(8,128)(2,1)} %get-tuple-element.117), channel_id=1, source_target_pairs={{10,0},{12,2},{14,4},{16,6},{18,8},{20,10},{22,12},{24,14},{26,16}... | collective-permute-start | bytes 983048 | tf_op jit(solution)/shard_map/ppermute | solution.py:555
  296.0 100.4 %collective-permute-start.22 = (bf16[640,384]{1,0:T(8,128)(2,1)}, bf16[640,384]{1,0:T(8,128)(2,1)}, u32[]{:S(2)}, u32[]{:S(2)}) collective-permute-start(bf16[640,384]{1,0:T(8,128)(2,1)} %select_convert_fusion.1), channel_id=1, source_target_pairs={{0,1},{1,0},{2,3},{3,2},{4,5},{5,4},{6,7},{7,6},{8,9},{9,8},{10,11... | collective-permute-start | bytes 1474568 | tf_op jit(solution)/shard_map/ppermute | solution.py:537
  299.2 32.7 %collective-permute-start.25 = (bf16[768,384]{1,0:T(8,128)(2,1)}, bf16[768,384]{1,0:T(8,128)(2,1)}, u32[]{:S(2)}, u32[]{:S(2)}) collective-permute-start(bf16[768,384]{1,0:T(8,128)(2,1)} %get-tuple-element.150), channel_id=1, source_target_pairs={{0,6},{2,4},{4,2},{6,0},{8,14},{10,12},{12,10},{14,8},{16,22},{18,... | collective-permute-start | bytes 1769480 | tf_op jit(solution)/shard_map/ppermute | solution.py:389
  306.5 37.2 %collective-permute-start.26 = (bf16[768,384]{1,0:T(8,128)(2,1)}, bf16[768,384]{1,0:T(8,128)(2,1)}, u32[]{:S(2)}, u32[]{:S(2)}) collective-permute-start(bf16[768,384]{1,0:T(8,128)(2,1)} %get-tuple-element.149), channel_id=1, source_target_pairs={{0,4},{2,6},{4,0},{6,2},{8,12},{10,14},{12,8},{14,10},{16,20},{18,... | collective-permute-start | bytes 1769480 | tf_op jit(solution)/shard_map/ppermute | solution.py:389
  306.5 37.2 %collective-permute-start.27 = (bf16[768,384]{1,0:T(8,128)(2,1)}, bf16[768,384]{1,0:T(8,128)(2,1)}, u32[]{:S(2)}, u32[]{:S(2)}) collective-permute-start(bf16[768,384]{1,0:T(8,128)(2,1)} %get-tuple-element.148), channel_id=1, source_target_pairs={{0,2},{2,0},{4,6},{6,4},{8,10},{10,8},{12,14},{14,12},{16,18},{18,... | collective-permute-start | bytes 1769480 | tf_op jit(solution)/shard_map/ppermute | solution.py:389
  365.9 29.5 %collective-permute-start.23 = (bf16[640,384]{1,0:T(8,128)(2,1)S(1)}, bf16[640,384]{1,0:T(8,128)(2,1)S(1)}, u32[]{:S(2)}, u32[]{:S(2)}) collective-permute-start(bf16[640,384]{1,0:T(8,128)(2,1)S(1)} %select_convert_fusion), channel_id=1, source_target_pairs={{0,1},{1,0},{2,3},{3,2},{4,5},{5,4},{6,7},{7,6},{8,9},{9,8},{10,11... | collective-permute-start | bytes 1474568 | tf_op jit(solution)/shard_map/ppermute | solution.py:537
  391.9 27.5 %collective-permute-start.35 = (bf16[784,384]{1,0:T(8,128)(2,1)S(1)}, bf16[784,384]{1,0:T(8,128)(2,1)S(1)}, u32[]{:S(2)}, u32[]{:S(2)}) collective-permute-start(bf16[784,384]{1,0:T(8,128)(2,1)S(1)} %pad_maximum_fusion.3), channel_id=1, source_target_pairs={{0,4},{2,6},{4,0},{6,2},{8,12},{10,14},{12,8},{14,10},{16,20},{18,... | collective-permute-start | bytes 1806344 | tf_op jit(solution)/shard_map/ppermute | solution.py:389
  393.8 25.7 %collective-permute-start.34 = (bf16[784,384]{1,0:T(8,128)(2,1)S(1)}, bf16[784,384]{1,0:T(8,128)(2,1)S(1)}, u32[]{:S(2)}, u32[]{:S(2)}) collective-permute-start(bf16[784,384]{1,0:T(8,128)(2,1)S(1)} %pad_maximum_fusion.3), channel_id=1, source_target_pairs={{0,6},{2,4},{4,2},{6,0},{8,14},{10,12},{12,10},{14,8},{16,22},{18,... | collective-permute-start | bytes 1806344 | tf_op jit(solution)/shard_map/ppermute | solution.py:389
  (58 other events, 704.2 us)
Sparse Core Ops, SparseCore 0:
  122.4 236.8 all-reduce.3

commit v3 on v2

--- a/solution.py
+++ b/solution.py
@@ -84,11 +84,12 @@
     high_start = jnp.clip(starts[-1] - place * tok_rows, 0, tok_rows)
     high_start = jnp.where(last[-1] > place, high_start, tok_rows)
     head_part = jnp.stack([low_end, high_start, place - base[-2], place - base[-1]])
-    return jnp.concatenate([head_part, rows, lengths]).astype(jnp.int32)
-
-
-def pack_kernel(heads, reach, table, proj, datt, gains, *outs):
-    slots, local = outs[:-1], outs[-1]
+    turns = jnp.remainder(-base[-2:], window)
+    return jnp.concatenate([head_part, rows, lengths, turns]).astype(jnp.int32)
+
+
+def pack_kernel(heads, spot, proj, datt, gains, local, *refs):
+    slots, sems = refs[:heads], refs[heads]
     rows = proj.shape[1]
     low = lax.broadcasted_iota(jnp.int32, (rows, 128), 1) < HS
     q_gain = gains[0:1, :] * (HS**-0.5)
@@ -104,14 +105,16 @@
         local[2 * pair, :, 128:256] = jnp.where(low, v, pltpu.roll(d, HS, 1)).astype(BF16)
         local[2 * pair + 1, :, 0:128] = jnp.where(low, pltpu.roll(q, HS, 1), k).astype(BF16)
         local[2 * pair + 1, :, 128:256] = jnp.where(low, pltpu.roll(v, HS, 1), d).astype(BF16)
-    low_end = table[0]
-    from_low = lax.broadcasted_iota(jnp.int32, (rows, 256), 0) < low_end
-    for index, slot in enumerate(slots):
-        distance = index - reach
-        low_head = jnp.clip(table[2] + distance, 0, heads - 1)
-        high_head = jnp.clip(table[3] + distance, 0, heads - 1)
-        picked = jnp.where(from_low, local[low_head].astype(F32), local[high_head].astype(F32))
-        slot[...] = picked.astype(BF16)
+
+    def copy_out(turn):
+        return pltpu.make_async_copy(
+            local.at[lax.rem(spot[0] + turn, heads)], slots[turn], sems.at[turn]
+        )
+
+    for turn in range(heads):
+        copy_out(turn).start()
+    for turn in range(heads):
+        copy_out(turn).wait()
 
 
 def softmax_tail(mixed, d_out):
@@ -297,10 +300,12 @@
             out[h, :, 128:256] = jnp.concatenate([d_key, d_value], axis=0).T.astype(BF16)
 
 
-def unpack_kernel(heads, reach, table, proj, gains, local, normed, cot, *refs):
+def unpack_kernel(heads, reach, table, spot, proj, gains, local, normed, cot, *refs):
     count = 2 * reach + 1
     backs = refs[:count]
-    attended, d_proj, gain_sums, grads, stacked, sems = refs[count:]
+    attended, d_proj, gain_sums = refs[count : count + 3]
+    blocks = refs[count + 3 : count + 7]
+    grads, stacked, sems = refs[count + 7 :]
     rows = proj.shape[1]
 
     def copy_in(b):
@@ -318,8 +323,8 @@
     k_gain = gains[1:2, :]
 
     def gathered(h):
-        lower = stacked[h - table[2] + reach].astype(F32)
-        upper = stacked[h - table[3] + reach].astype(F32)
+        lower = stacked[lax.rem(h + table[4 + 4 * reach], heads) - table[2] + reach].astype(F32)
+        upper = stacked[lax.rem(h + table[5 + 4 * reach], heads) - table[3] + reach].astype(F32)
         return jnp.where(from_low, lower, jnp.where(from_high, upper, local[h].astype(F32)))
 
     def back(raw, gradient, gain):
@@ -347,12 +352,19 @@
         d_proj[2, :, lanes] = d_value.astype(BF16)
     gain_sums[...] = jnp.concatenate([q_sum * (HS**-0.5), k_sum], axis=0)
     width, columns = normed.shape[1], heads * HS
-    for part in range(3):
-        grads[part * width : (part + 1) * width, :] = dot_tn(normed[...], d_proj[part]).astype(BF16)
-    for part in range(width // columns):
-        at = 3 * width + part * columns
-        lanes = slice(part * columns, (part + 1) * columns)
-        grads[at : at + columns, :] = dot_tn(attended[...], cot[:, lanes]).astype(BF16)
+
+    for part in range(4):
+        if part < 3:
+            grads[part] = dot_tn(normed[...], d_proj[part]).astype(BF16)
+        else:
+            for at in range(0, width, columns):
+                grads[part, at : at + columns, :] = dot_tn(
+                    attended[...], cot[:, at : at + columns]
+                ).astype(BF16)
+    for index, block in enumerate(blocks):
+        pltpu.make_async_copy(grads.at[index ^ spot[0]], block, sems.at[index]).start()
+    for index, block in enumerate(blocks):
+        pltpu.make_async_copy(grads.at[index ^ spot[0]], block, sems.at[index]).wait()
 
 
 class SeqSum:
@@ -363,7 +375,7 @@
         self.order = stages + stages[::-1]
         self.phases = len(self.order)
         self.codes = {bit: (place >> bit) & (radix - 1) for bit, radix in stages}
-        self.current, self.small = blocks, small
+        self.blocks, self.current, self.small = blocks, None, small
 
     def describe(self, phase):
         bit, radix = self.order[phase]
@@ -371,9 +383,13 @@
         joins = self.small is not None and adding == (bit > 0)
         return bit, radix, adding, joins, self.codes[bit]
 
-    def split(self, radix):
+    def block(self, phase, mask):
+        bit, radix, _, _, code = self.describe(phase)
+        if phase == 0:
+            return self.blocks[mask]
         rows, lanes = self.current.shape
-        return self.current.reshape(radix, rows // radix, lanes)
+        split = self.current.reshape(radix, rows // radix, lanes)
+        return lax.dynamic_index_in_dim(split, code ^ mask, 0, keepdims=False)
 
     def send(self, phase):
         bit, radix, adding, joins, code = self.describe(phase)
@@ -382,7 +398,7 @@
         for mask in reversed(range(1, radix)):
             block = self.current
             if adding:
-                block = lax.dynamic_index_in_dim(self.split(radix), code ^ mask, 0, keepdims=False)
+                block = self.block(phase, mask)
             if joins:
                 block = jnp.concatenate([block, tail], axis=0)
             route = [(i, i ^ (mask << bit)) for i in range(self.n_seq)]
@@ -391,10 +407,10 @@
 
     def receive(self, phase, arrived):
         bit, radix, adding, joins, code = self.describe(phase)
-        rows, lanes = self.current.shape
-        height = rows // radix if adding else rows
+        own = self.block(phase, 0) if adding else self.current
+        height, lanes = own.shape
         if adding:
-            total = lax.dynamic_index_in_dim(self.split(radix), code, 0, keepdims=False).astype(F32)
+            total = own.astype(F32)
             for block in arrived:
                 total = total + block[:height].astype(F32)
             self.current = total.astype(BF16)
@@ -433,18 +449,18 @@
     )
 
 
-def pack(heads, reach, table, proj, datt, gains):
+def pack(heads, spot, proj, datt, gains):
     rows = proj.shape[1]
     slot = jax.ShapeDtypeStruct((rows, 4 * HS), BF16)
-    count = 2 * reach + 1
     return pl.pallas_call(
-        functools.partial(pack_kernel, heads, reach),
-        out_shape=[slot] * count + [jax.ShapeDtypeStruct((heads, rows, 4 * HS), BF16)],
+        functools.partial(pack_kernel, heads),
+        out_shape=[jax.ShapeDtypeStruct((heads, rows, 4 * HS), BF16)] + [slot] * heads,
         in_specs=[in_smem(), in_vmem(), in_vmem(), in_vmem()],
-        out_specs=[in_vmem()] * (count + 1),
+        out_specs=[in_vmem()] + [anywhere()] * heads,
+        scratch_shapes=[pltpu.SemaphoreType.DMA((heads,))],
         compiler_params=compiler_params(),
         cost_estimate=cost(10**9, 10**7),
-    )(table, proj, datt, gains)
+    )(spot, proj, datt, gains)
 
 
 def work(reach, tok_rows, table, blocks):
@@ -486,7 +502,7 @@
     )(table, local, ids_row, ids_column)
 
 
-def unpack(heads, reach, table, proj, gains, local, normed, cot, backs):
+def unpack(heads, reach, table, spot, proj, gains, local, normed, cot, backs):
     rows = proj.shape[1]
     count = 2 * reach + 1
     width = heads * HS
@@ -496,17 +512,18 @@
             jax.ShapeDtypeStruct((rows, width), BF16),
             jax.ShapeDtypeStruct((3, rows, width), BF16),
             jax.ShapeDtypeStruct((2, 128), F32),
-            jax.ShapeDtypeStruct((4 * normed.shape[1], width), BF16),
-        ],
-        in_specs=[in_smem()] + [in_vmem()] * 5 + [anywhere()] * count,
-        out_specs=[in_vmem()] * 4,
+        ]
+        + [jax.ShapeDtypeStruct((normed.shape[1], width), BF16)] * 4,
+        in_specs=[in_smem()] * 2 + [in_vmem()] * 5 + [anywhere()] * count,
+        out_specs=[in_vmem()] * 3 + [anywhere()] * 4,
         scratch_shapes=[
+            pltpu.VMEM((4, normed.shape[1], width), BF16),
             pltpu.VMEM((count, rows, 4 * HS), BF16),
             pltpu.SemaphoreType.DMA((count,)),
         ],
         compiler_params=compiler_params(),
         cost_estimate=cost(10**9, 10**7),
-    )(table, proj, gains, local, normed, cot, *backs)
+    )(table, spot, proj, gains, local, normed, cot, *backs)
 
 
 def on_device(
@@ -554,6 +571,20 @@
         route = [(i, i + distance) for i in range(n_seq) if 0 <= i + distance < n_seq]
         return lax.ppermute(block, "seq", route)
 
+    gains = jnp.tile(jnp.stack([q_gain, k_gain]), (1, 2))
+
+    gathered = both_halves(tokens)
+    cot_whole = both_halves(cotangent)
+    normed_f, norm_pull = jax.vjp(layer_norm, gathered.astype(F32), ln_gain)
+    normed = normed_f.astype(BF16)
+    proj = jnp.einsum("td,dkc->ktc", normed, w_qkv, preferred_element_type=F32)
+    d_attended = jnp.einsum("td,cd->tc", cot_whole, w_attn_out, preferred_element_type=F32)
+    spot = jnp.reshape(place, (1,)).astype(jnp.int32)
+    packed = pack(heads, spot, proj, d_attended.astype(BF16), gains)
+    packed, image_starts = lax.optimization_barrier((packed, image_starts))
+    local, slots = packed[0], packed[1:]
+
+    arrived = [shifted(slots[d % heads], d) for d in range(reach, -reach - 1, -1)]
     table = work_table(image_starts, place, n_seq, tok_rows, reach)
     row_index = jnp.arange(tok_rows, dtype=jnp.int32)
     positions = place * tok_rows + row_index
@@ -561,20 +592,8 @@
     is_local = (row_index >= table[0]) & (row_index < table[1])
     ids_column = jnp.where(is_local, ids, -1)[:, None]
     ids_row = jnp.where(is_local, ids, -2)[None, :]
-    gains = jnp.tile(jnp.stack([q_gain, k_gain]), (1, 2))
-
-    gathered = both_halves(tokens)
-    cot_whole = both_halves(cotangent)
-    normed_f, norm_pull = jax.vjp(layer_norm, gathered.astype(F32), ln_gain)
-    normed = normed_f.astype(BF16)
-    proj = jnp.einsum("td,dkc->ktc", normed, w_qkv, preferred_element_type=F32)
-    d_attended = jnp.einsum("td,cd->tc", cot_whole, w_attn_out, preferred_element_type=F32)
-    packed = pack(heads, reach, table, proj, d_attended.astype(BF16), gains)
-    packed, normed_ff, cot_ff = lax.optimization_barrier((packed, normed, cot_whole))
-    slots, local = packed[:-1], packed[-1]
-
-    arrived = [shifted(slots[reach + d], d) for d in range(reach, -reach - 1, -1)]
-
+
+    arrived[0], normed_ff, cot_ff = lax.optimization_barrier((arrived[0], normed, cot_whole))
     up_input = jnp.dot(normed_ff, w_up, preferred_element_type=F32) + up_bias
     hidden_f, gelu_pull = jax.vjp(exact_gelu, up_input)
     hidden = hidden_f.astype(BF16)
@@ -586,16 +605,17 @@
     grad_out_bias = jnp.sum(cotangent.astype(F32), axis=0)
     grad_up_bias = jnp.sum(d_upper.astype(F32), axis=0)
     early = (grad_down.astype(BF16), grad_up.astype(BF16))
-    early, arrived = lax.optimization_barrier((early, arrived))
     early = lax.psum(early, "seq")
     ffn_out = jnp.dot(hidden, w_down, preferred_element_type=F32)
     ffn_back = jnp.einsum("tf,df->td", d_upper, w_up, preferred_element_type=F32)
 
+    worked = list(work(reach, tok_rows, table, arrived))
+    worked[0], local = lax.optimization_barrier((worked[0], local))
     local_out = local_work(heads, table, local, ids_row, ids_column)
-    worked = work(reach, tok_rows, table, arrived)
     returned = [shifted(worked[b], b - reach) for b in range(2 * reach + 1)][::-1]
-    attended, d_proj, gain_sums, late = unpack(
-        heads, reach, table, proj, gains, local_out, normed, cot_whole, returned
+    corner = jnp.bitwise_and(spot, 3)
+    attended, d_proj, gain_sums, *late = unpack(
+        heads, reach, table, corner, proj, gains, local_out, normed, cot_whole, returned
     )
 
     partial_out = jnp.dot(attended, w_attn_out, preferred_element_type=F32) + ffn_out

time: 445 us -> 444 us (level); the launches traced: 437 us -> 442 us
  starting transfers between devices: 108 us -> 141 us
  waiting for transfers between devices: 130 us -> 112 us
  Pallas kernels: 94.5 us -> 81.1 us
    ppermute x12, starting transfers between devices: 20.4 us -> 50.5 us  [send(): arrived.append(lax.ppermute(block, 'seq', route))]
    psum x1, waiting for transfers between devices: 15.5 us -> 0.01 us  [on_device(): early = lax.psum(early, 'seq')]
    pallas_call x1, Pallas kernels: 28 us -> 12.8 us  [local_work(): pl.pallas_call(functools.partial(local_kernel, heads), out_shape=jax.Shap...]
    ppermute x12, waiting for transfers between devices: 70.7 us -> 57.5 us  [send(): arrived.append(lax.ppermute(block, 'seq', route))]
    ppermute x20, waiting for transfers between devices: 44 us -> 54.4 us  [shifted(): return lax.ppermute(block, 'seq', route)]
  transfers between devices with their start and end apart: 38 -> 38, of which waited for: 16 -> 16; matrix products, arithmetic and copies ran while one was open for 10% -> 14% of each run, Pallas kernels for 20% -> 17%
where the time goes in v3:
time: 444 us; the launch traced here: 442 us
  starting transfers between devices  141 us (32%)
  waiting for transfers between devices  112 us (25%)
  Pallas kernels  81.1 us (18%)
  matrix products  38.4 us (9%)
  other arithmetic  27.2 us (6%)
  local copies, waits for them, and re-layouts  22.5 us (5%)
  between operations  19.5 us (4%)
    ppermute x20, starting transfers between devices, shifted(): return lax.ppermute(block, 'seq', route)  89.5 us
    ppermute x12, waiting for transfers between devices, send(): arrived.append(lax.ppermute(block, 'seq', route))  57.5 us
    ppermute x20, waiting for transfers between devices, shifted(): return lax.ppermute(block, 'seq', route)  54.4 us
    ppermute x12, starting transfers between devices, send(): arrived.append(lax.ppermute(block, 'seq', route))  50.5 us
    pallas_call x1, Pallas kernels, work(): pl.pallas_call(functools.partial(work_kernel, reach, tok_rows, max_tiles)...  47.7 us
    pallas_call x1, Pallas kernels, unpack(): pl.pallas_call(functools.partial(unpack_kernel, heads, reach), out_shape=...  14.5 us
    pallas_call x1, Pallas kernels, local_work(): pl.pallas_call(functools.partial(local_kernel, heads), out_shape=jax.Shap...  12.8 us
    dot_general x1, matrix products, on_device(): jnp.einsum('td,fd->tf', cot_ff, w_down, preferred_element_type=F32)  10.8 us
  transfers between devices with their start and end apart: 38, of which 16 were waited for; matrix products, arithmetic and copies ran while one was open for 14% of the time, Pallas kernels for 17%

profile of v3, /device:TPU:0, one launch (start us, length us, event | category | flops | bytes accessed | tf_op | source)
XLA Modules:
  0.0 441.8 jit_solution(17630703312367393746)
XLA Ops:
  18.6 6.2 %shard_map.203 = (bf16[6,640,256]{2,1,0:T(8,128)(2,1)}, bf16[640,256]{1,0:T(8,128)(2,1)}, bf16[640,256]{1,0:T(8,128)(2,1)}, bf16[640,256]{1,0:T(8,128)(2,1)}, bf...) custom-call(s32[1]{0:T(128)} %bitcast.spot, ...), custom_call_target="tpu_custom_call" | custom-call | flops 1000000000 | bytes 10000000 | tf_op jit(solution)/shard_map/pallas_call | solution.py:455
  28.1 6.5 %collective-permute-start.2 = (bf16[640,256]{1,0:T(8,128)(2,1)}, bf16[640,256]{1,0:T(8,128)(2,1)}, u32[]{:S(2)}, u32[]{:S(2)}) collective-permute-start(bf16[640,256]{1,0:T(8,128)(2,1)} %get-tuple-element.62), channel_id=1, source_target_pairs={{0,10},{2,12},{4,14},{6,16},{8,18},{10,20},{12,22},{14,24},{16,26}... | collective-permute-start | bytes 983048 | tf_op jit(solution)/shard_map/ppermute | solution.py:572
  40.4 7.2 %collective-permute-start.3 = (bf16[640,256]{1,0:T(8,128)(2,1)}, bf16[640,256]{1,0:T(8,128)(2,1)}, u32[]{:S(2)}, u32[]{:S(2)}) collective-permute-start(bf16[640,256]{1,0:T(8,128)(2,1)} %get-tuple-element.64), channel_id=1, source_target_pairs={{0,8},{2,10},{4,12},{6,14},{8,16},{10,18},{12,20},{14,22},{16,24},... | collective-permute-start | bytes 983048 | tf_op jit(solution)/shard_map/ppermute | solution.py:572
  61.3 3.7 fusion.37
  65.0 10.8 %fusion.30 = (bf16[1536]{0:T(1024)(128)(2,1)S(1)}, bf16[640,1536]{1,0:T(8,128)(2,1)S(1)}, f32[640,1536]{1,0:T(8,128)S(1)}) fusion(f32[640,1536]{1,0:T(8,128)S(1)} %fusion.37, f32[1536]{0:T(1024)S(1)} %copy-done.27, bf16[640,768]{1,0:T(8,128)(2,1)S(1)} %pad_maximum_fusion.2.cot, bf16[1536,768]{1,0:T(8,128)(2,1)S(1)} %copy-done), kind=kOutput, calls=%fused_computation.110 | convolution fusion | flops 1582692864 | bytes 13181952 | tf_op jit(solution)/shard_map/td,fd->tf/dot_general | solution.py:600
  89.3 8.3 %collective-permute-done.8.refs_7_ = bf16[640,256]{1,0:T(8,128)(2,1)} collective-permute-done((bf16[640,256]{1,0:T(8,128)(2,1)}, bf16[640,256]{1,0:T(8,128)(2,1)}, u32[]{:S(2)}, u32[]{:S(2)}) %collective-permute-start.8) | collective-permute-done | bytes 327712 | tf_op jit(solution)/shard_map/ppermute | solution.py:572
  97.7 6.5 %collective-permute-done.10.refs_9_ = bf16[640,256]{1,0:T(8,128)(2,1)} collective-permute-done((bf16[640,256]{1,0:T(8,128)(2,1)}, bf16[640,256]{1,0:T(8,128)(2,1)}, u32[]{:S(2)}, u32[]{:S(2)}) %collective-permute-start.10) | collective-permute-done | bytes 327712 | tf_op jit(solution)/shard_map/ppermute | solution.py:572
  104.2 21.8 %collective-permute-done.11.refs_10_ = bf16[640,256]{1,0:T(8,128)(2,1)} collective-permute-done((bf16[640,256]{1,0:T(8,128)(2,1)}, bf16[640,256]{1,0:T(8,128)(2,1)}, u32[]{:S(2)}, u32[]{:S(2)}) %collective-permute-start.11) | collective-permute-done | bytes 327712 | tf_op jit(solution)/shard_map/ppermute | solution.py:572
  126.0 47.7 %shard_map.204 = (bf16[640,256]{1,0:T(8,128)(2,1)}, bf16[640,256]{1,0:T(8,128)(2,1)}, bf16[640,256]{1,0:T(8,128)(2,1)}, bf16[640,256]{1,0:T(8,128)(2,1)}, bf16[6...) custom-call(s32[26]{0:T(128)} %concatenate.42.table, ...), custom_call_target="tpu_custom_call" | custom-call | flops 30000001024 | bytes 10000000 | tf_op jit(solution)/shard_map/pallas_call | solution.py:471
  178.0 24.4 %collective-permute-start.14 = (bf16[640,256]{1,0:T(8,128)(2,1)}, bf16[640,256]{1,0:T(8,128)(2,1)}, u32[]{:S(2)}, u32[]{:S(2)}) collective-permute-start(bf16[640,256]{1,0:T(8,128)(2,1)} %get-tuple-element.74), channel_id=1, source_target_pairs={{0,6},{2,8},{4,10},{6,12},{8,14},{10,16},{12,18},{14,20},{16,22},{... | collective-permute-start | bytes 983048 | tf_op jit(solution)/shard_map/ppermute | solution.py:572
  202.4 22.2 %collective-permute-start.15 = (bf16[640,256]{1,0:T(8,128)(2,1)}, bf16[640,256]{1,0:T(8,128)(2,1)}, u32[]{:S(2)}, u32[]{:S(2)}) collective-permute-start(bf16[640,256]{1,0:T(8,128)(2,1)} %get-tuple-element.75), channel_id=1, source_target_pairs={{0,4},{2,6},{4,8},{6,10},{8,12},{10,14},{12,16},{14,18},{16,20},{1... | collective-permute-start | bytes 983048 | tf_op jit(solution)/shard_map/ppermute | solution.py:572
  226.8 4.6 %fusion.38 = f32[640,768]{1,0:T(8,128)} fusion(bf16[640,1536]{1,0:T(8,128)(2,1)} %copy-done.12, bf16[1536,768]{1,0:T(8,128)(2,1)S(1)} %copy-done), kind=kOutput, calls=%fused_computation.117 | convolution fusion | flops 1509949440 | bytes 6291456 | tf_op jit(solution)/shard_map/dot_general | solution.py:609
  241.0 12.8 %shard_map.205.local = bf16[6,640,256]{2,1,0:T(8,128)(2,1)} custom-call(s32[26]{0:T(128)} %concatenate.42.table, bf16[6,640,256]{2,1,0:T(8,128)(2,1)} %get-tuple-element.71.local, s32[1,640]{1,0:T(1,128)} %and_select_fusion.ids_row, s32[640,1]{1,0:T(8,128)} %reshape_select_fusion.ids_column), custom_call_target="tpu_custom_call" | custom-call | flops 5000000000 | bytes 4000000 | tf_op jit(solution)/shard_map/pallas_call | solution.py:495
  254.7 13.1 %collective-permute-done.20.refs_9_ = bf16[640,256]{1,0:T(8,128)(2,1)} collective-permute-done((bf16[640,256]{1,0:T(8,128)(2,1)}, bf16[640,256]{1,0:T(8,128)(2,1)}, u32[]{:S(2)}, u32[]{:S(2)}) %collective-permute-start.20) | collective-permute-done | bytes 327712 | tf_op jit(solution)/shard_map/ppermute | solution.py:572
  271.4 14.5 %shard_map.206 = (bf16[640,384]{1,0:T(8,128)(2,1)}, bf16[3,640,384]{2,1,0:T(8,128)(2,1)}, f32[2,128]{1,0:T(2,128)}, bf16[768,384]{1,0:T(8,128)(2,1)}, bf16[768,3...) custom-call(s32[26]{0:T(128)} %concatenate.42.table, s32[1]{0:T(128)S(6)} %and.64.spot, ...), custom_call_target="tpu_custom_call" | custom-call | flops 1000000000 | bytes 10000000 | tf_op jit(solution)/shard_map/pallas_call | solution.py:509
  285.9 4.2 fusion.15
  295.7 37.4 %collective-permute-start.25 = (bf16[768,384]{1,0:T(8,128)(2,1)}, bf16[768,384]{1,0:T(8,128)(2,1)}, u32[]{:S(2)}, u32[]{:S(2)}) collective-permute-start(bf16[768,384]{1,0:T(8,128)(2,1)} %get-tuple-element.89), channel_id=1, source_target_pairs={{0,6},{2,4},{4,2},{6,0},{8,14},{10,12},{12,10},{14,8},{16,22},{18,... | collective-permute-start | bytes 1769480 | tf_op jit(solution)/shard_map/ppermute | solution.py:405
  337.4 10.3 %collective-permute-done.25 = bf16[768,384]{1,0:T(8,128)(2,1)} collective-permute-done((bf16[768,384]{1,0:T(8,128)(2,1)}, bf16[768,384]{1,0:T(8,128)(2,1)}, u32[]{:S(2)}, u32[]{:S(2)}) %collective-permute-start.25) | collective-permute-done | bytes 589856 | tf_op jit(solution)/shard_map/ppermute | solution.py:405
  347.7 12.4 %collective-permute-done.26 = bf16[768,384]{1,0:T(8,128)(2,1)} collective-permute-done((bf16[768,384]{1,0:T(8,128)(2,1)}, bf16[768,384]{1,0:T(8,128)(2,1)}, u32[]{:S(2)}, u32[]{:S(2)}) %collective-permute-start.26) | collective-permute-done | bytes 589856 | tf_op jit(solution)/shard_map/ppermute | solution.py:405
  362.4 4.3 collective-permute-start.28
  369.6 7.5 %collective-permute-done.29 = bf16[208,384]{1,0:T(8,128)(2,1)S(1)} collective-permute-done((bf16[208,384]{1,0:T(8,128)(2,1)S(1)}, bf16[208,384]{1,0:T(8,128)(2,1)S(1)}, u32[]{:S(2)}, u32[]{:S(2)}) %collective-permute-start.29) | collective-permute-done | bytes 159776 | tf_op jit(solution)/shard_map/ppermute | solution.py:405
  381.9 4.2 collective-permute-done.31
  386.1 6.6 %collective-permute-done.32 = bf16[192,384]{1,0:T(8,128)(2,1)S(1)} collective-permute-done((bf16[192,384]{1,0:T(8,128)(2,1)S(1)}, bf16[192,384]{1,0:T(8,128)(2,1)S(1)}, u32[]{:S(2)}, u32[]{:S(2)}) %collective-permute-start.32) | collective-permute-done | bytes 147488 | tf_op jit(solution)/shard_map/ppermute | solution.py:405
  409.4 11.8 %collective-permute-done.35 = bf16[784,384]{1,0:T(8,128)(2,1)S(1)} collective-permute-done((bf16[784,384]{1,0:T(8,128)(2,1)S(1)}, bf16[784,384]{1,0:T(8,128)(2,1)S(1)}, u32[]{:S(2)}, u32[]{:S(2)}) %collective-permute-start.35) | collective-permute-done | bytes 602144 | tf_op jit(solution)/shard_map/ppermute | solution.py:405
  (214 shorter events, 113.3 us)
Async XLA Ops:
  7.2 352.9 %all-reduce.4.cloned.1.call-start = ((), (), s32[]{:S(2)}) async-start(), calls=%async_computation | async-start | bytes 9437184 | tf_op jit(solution)/shard_map/psum | solution.py:608
  28.1 29.6 %collective-permute-start.2 = (bf16[640,256]{1,0:T(8,128)(2,1)}, bf16[640,256]{1,0:T(8,128)(2,1)}, u32[]{:S(2)}, u32[]{:S(2)}) collective-permute-start(bf16[640,256]{1,0:T(8,128)(2,1)} %get-tuple-element.62), channel_id=1, source_target_pairs={{0,10},{2,12},{4,14},{6,16},{8,18},{10,20},{12,22},{14,24},{16,26}... | collective-permute-start | bytes 983048 | tf_op jit(solution)/shard_map/ppermute | solution.py:572
  34.6 54.7 %collective-permute-start.7 = (bf16[640,256]{1,0:T(8,128)(2,1)}, bf16[640,256]{1,0:T(8,128)(2,1)}, u32[]{:S(2)}, u32[]{:S(2)}) collective-permute-start(bf16[640,256]{1,0:T(8,128)(2,1)} %get-tuple-element.62), channel_id=1, source_target_pairs={{2,0},{4,2},{6,4},{8,6},{10,8},{12,10},{14,12},{16,14},{18,16},{20... | collective-permute-start | bytes 983048 | tf_op jit(solution)/shard_map/ppermute | solution.py:572
  40.4 39.9 %collective-permute-start.3 = (bf16[640,256]{1,0:T(8,128)(2,1)}, bf16[640,256]{1,0:T(8,128)(2,1)}, u32[]{:S(2)}, u32[]{:S(2)}) collective-permute-start(bf16[640,256]{1,0:T(8,128)(2,1)} %get-tuple-element.64), channel_id=1, source_target_pairs={{0,8},{2,10},{4,12},{6,14},{8,16},{10,18},{12,20},{14,22},{16,24},... | collective-permute-start | bytes 983048 | tf_op jit(solution)/shard_map/ppermute | solution.py:572
  47.6 34.1 %collective-permute-start.4 = (bf16[640,256]{1,0:T(8,128)(2,1)}, bf16[640,256]{1,0:T(8,128)(2,1)}, u32[]{:S(2)}, u32[]{:S(2)}) collective-permute-start(bf16[640,256]{1,0:T(8,128)(2,1)} %get-tuple-element.65), channel_id=1, source_target_pairs={{0,6},{2,8},{4,10},{6,12},{8,14},{10,16},{12,18},{14,20},{16,22},{... | collective-permute-start | bytes 983048 | tf_op jit(solution)/shard_map/ppermute | solution.py:572
  50.2 33.0 %collective-permute-start.5 = (bf16[640,256]{1,0:T(8,128)(2,1)}, bf16[640,256]{1,0:T(8,128)(2,1)}, u32[]{:S(2)}, u32[]{:S(2)}) collective-permute-start(bf16[640,256]{1,0:T(8,128)(2,1)} %get-tuple-element.66), channel_id=1, source_target_pairs={{0,4},{2,6},{4,8},{6,10},{8,12},{10,14},{12,16},{14,18},{16,20},{1... | collective-permute-start | bytes 983048 | tf_op jit(solution)/shard_map/ppermute | solution.py:572
  57.8 26.8 %collective-permute-start.6 = (bf16[640,256]{1,0:T(8,128)(2,1)}, bf16[640,256]{1,0:T(8,128)(2,1)}, u32[]{:S(2)}, u32[]{:S(2)}) collective-permute-start(bf16[640,256]{1,0:T(8,128)(2,1)} %get-tuple-element.67), channel_id=1, source_target_pairs={{0,2},{2,4},{4,6},{6,8},{8,10},{10,12},{12,14},{14,16},{16,18},{18... | collective-permute-start | bytes 983048 | tf_op jit(solution)/shard_map/ppermute | solution.py:572
  83.2 21.0 %collective-permute-start.10 = (bf16[640,256]{1,0:T(8,128)(2,1)}, bf16[640,256]{1,0:T(8,128)(2,1)}, u32[]{:S(2)}, u32[]{:S(2)}) collective-permute-start(bf16[640,256]{1,0:T(8,128)(2,1)} %get-tuple-element.66), channel_id=1, source_target_pairs={{8,0},{10,2},{12,4},{14,6},{16,8},{18,10},{20,12},{22,14},{24,16},... | collective-permute-start | bytes 983048 | tf_op jit(solution)/shard_map/ppermute | solution.py:572
  84.5 41.5 %collective-permute-start.11 = (bf16[640,256]{1,0:T(8,128)(2,1)}, bf16[640,256]{1,0:T(8,128)(2,1)}, u32[]{:S(2)}, u32[]{:S(2)}) collective-permute-start(bf16[640,256]{1,0:T(8,128)(2,1)} %get-tuple-element.67), channel_id=1, source_target_pairs={{10,0},{12,2},{14,4},{16,6},{18,8},{20,10},{22,12},{24,14},{26,16}... | collective-permute-start | bytes 983048 | tf_op jit(solution)/shard_map/ppermute | solution.py:572
  173.7 60.8 %collective-permute-start.12 = (bf16[640,256]{1,0:T(8,128)(2,1)}, bf16[640,256]{1,0:T(8,128)(2,1)S(1)}, u32[]{:S(2)}, u32[]{:S(2)}) collective-permute-start(bf16[640,256]{1,0:T(8,128)(2,1)} %get-tuple-element.72), channel_id=1, source_target_pairs={{0,10},{2,12},{4,14},{6,16},{8,18},{10,20},{12,22},{14,24},{16,26}... | collective-permute-start | bytes 983048 | tf_op jit(solution)/shard_map/ppermute | solution.py:572
  176.7 59.0 %collective-permute-start.13 = (bf16[640,256]{1,0:T(8,128)(2,1)}, bf16[640,256]{1,0:T(8,128)(2,1)S(1)}, u32[]{:S(2)}, u32[]{:S(2)}) collective-permute-start(bf16[640,256]{1,0:T(8,128)(2,1)} %get-tuple-element.73), channel_id=1, source_target_pairs={{0,8},{2,10},{4,12},{6,14},{8,16},{10,18},{12,20},{14,22},{16,24},... | collective-permute-start | bytes 983048 | tf_op jit(solution)/shard_map/ppermute | solution.py:572
  178.0 59.0 %collective-permute-start.14 = (bf16[640,256]{1,0:T(8,128)(2,1)}, bf16[640,256]{1,0:T(8,128)(2,1)}, u32[]{:S(2)}, u32[]{:S(2)}) collective-permute-start(bf16[640,256]{1,0:T(8,128)(2,1)} %get-tuple-element.74), channel_id=1, source_target_pairs={{0,6},{2,8},{4,10},{6,12},{8,14},{10,16},{12,18},{14,20},{16,22},{... | collective-permute-start | bytes 983048 | tf_op jit(solution)/shard_map/ppermute | solution.py:572
  202.4 36.0 %collective-permute-start.15 = (bf16[640,256]{1,0:T(8,128)(2,1)}, bf16[640,256]{1,0:T(8,128)(2,1)}, u32[]{:S(2)}, u32[]{:S(2)}) collective-permute-start(bf16[640,256]{1,0:T(8,128)(2,1)} %get-tuple-element.75), channel_id=1, source_target_pairs={{0,4},{2,6},{4,8},{6,10},{8,12},{10,14},{12,16},{14,18},{16,20},{1... | collective-permute-start | bytes 983048 | tf_op jit(solution)/shard_map/ppermute | solution.py:572
  234.4 19.3 %collective-permute-start.17 = (bf16[640,256]{1,0:T(8,128)(2,1)}, bf16[640,256]{1,0:T(8,128)(2,1)}, u32[]{:S(2)}, u32[]{:S(2)}) collective-permute-start(bf16[640,256]{1,0:T(8,128)(2,1)} %get-tuple-element.78), channel_id=1, source_target_pairs={{2,0},{4,2},{6,4},{8,6},{10,8},{12,10},{14,12},{16,14},{18,16},{20... | collective-permute-start | bytes 983048 | tf_op jit(solution)/shard_map/ppermute | solution.py:572
  235.7 18.0 %collective-permute-start.18 = (bf16[640,256]{1,0:T(8,128)(2,1)}, bf16[640,256]{1,0:T(8,128)(2,1)}, u32[]{:S(2)}, u32[]{:S(2)}) collective-permute-start(bf16[640,256]{1,0:T(8,128)(2,1)} %get-tuple-element.79), channel_id=1, source_target_pairs={{4,0},{6,2},{8,4},{10,6},{12,8},{14,10},{16,12},{18,14},{20,16},{2... | collective-permute-start | bytes 983048 | tf_op jit(solution)/shard_map/ppermute | solution.py:572
  238.4 29.5 %collective-permute-start.20 = (bf16[640,256]{1,0:T(8,128)(2,1)}, bf16[640,256]{1,0:T(8,128)(2,1)}, u32[]{:S(2)}, u32[]{:S(2)}) collective-permute-start(bf16[640,256]{1,0:T(8,128)(2,1)} %get-tuple-element.81), channel_id=1, source_target_pairs={{8,0},{10,2},{12,4},{14,6},{16,8},{18,10},{20,12},{22,14},{24,16},... | collective-permute-start | bytes 983048 | tf_op jit(solution)/shard_map/ppermute | solution.py:572
  239.7 31.7 %collective-permute-start.21 = (bf16[640,256]{1,0:T(8,128)(2,1)}, bf16[640,256]{1,0:T(8,128)(2,1)}, u32[]{:S(2)}, u32[]{:S(2)}) collective-permute-start(bf16[640,256]{1,0:T(8,128)(2,1)} %get-tuple-element.82), channel_id=1, source_target_pairs={{10,0},{12,2},{14,4},{16,6},{18,8},{20,10},{22,12},{24,14},{26,16}... | collective-permute-start | bytes 983048 | tf_op jit(solution)/shard_map/ppermute | solution.py:572
  295.4 102.0 %collective-permute-start.22 = (bf16[640,384]{1,0:T(8,128)(2,1)}, bf16[640,384]{1,0:T(8,128)(2,1)}, u32[]{:S(2)}, u32[]{:S(2)}) collective-permute-start(bf16[640,384]{1,0:T(8,128)(2,1)} %select_convert_fusion.1), channel_id=1, source_target_pairs={{0,1},{1,0},{2,3},{3,2},{4,5},{5,4},{6,7},{7,6},{8,9},{9,8},{10,11... | collective-permute-start | bytes 1474568 | tf_op jit(solution)/shard_map/ppermute | solution.py:554
  295.7 51.9 %collective-permute-start.25 = (bf16[768,384]{1,0:T(8,128)(2,1)}, bf16[768,384]{1,0:T(8,128)(2,1)}, u32[]{:S(2)}, u32[]{:S(2)}) collective-permute-start(bf16[768,384]{1,0:T(8,128)(2,1)} %get-tuple-element.89), channel_id=1, source_target_pairs={{0,6},{2,4},{4,2},{6,0},{8,14},{10,12},{12,10},{14,8},{16,22},{18,... | collective-permute-start | bytes 1769480 | tf_op jit(solution)/shard_map/ppermute | solution.py:405
  333.1 27.0 %collective-permute-start.26 = (bf16[768,384]{1,0:T(8,128)(2,1)}, bf16[768,384]{1,0:T(8,128)(2,1)}, u32[]{:S(2)}, u32[]{:S(2)}) collective-permute-start(bf16[768,384]{1,0:T(8,128)(2,1)} %get-tuple-element.90), channel_id=1, source_target_pairs={{0,4},{2,6},{4,0},{6,2},{8,12},{10,14},{12,8},{14,10},{16,20},{18,... | collective-permute-start | bytes 1769480 | tf_op jit(solution)/shard_map/ppermute | solution.py:405
  333.1 27.0 %collective-permute-start.27 = (bf16[768,384]{1,0:T(8,128)(2,1)}, bf16[768,384]{1,0:T(8,128)(2,1)}, u32[]{:S(2)}, u32[]{:S(2)}) collective-permute-start(bf16[768,384]{1,0:T(8,128)(2,1)} %get-tuple-element.91), channel_id=1, source_target_pairs={{0,2},{2,0},{4,6},{6,4},{8,10},{10,8},{12,14},{14,12},{16,18},{18,... | collective-permute-start | bytes 1769480 | tf_op jit(solution)/shard_map/ppermute | solution.py:405
  366.8 29.7 %collective-permute-start.23 = (bf16[640,384]{1,0:T(8,128)(2,1)S(1)}, bf16[640,384]{1,0:T(8,128)(2,1)S(1)}, u32[]{:S(2)}, u32[]{:S(2)}) collective-permute-start(bf16[640,384]{1,0:T(8,128)(2,1)S(1)} %select_convert_fusion), channel_id=1, source_target_pairs={{0,1},{1,0},{2,3},{3,2},{4,5},{5,4},{6,7},{7,6},{8,9},{9,8},{10,11... | collective-permute-start | bytes 1474568 | tf_op jit(solution)/shard_map/ppermute | solution.py:554
  394.1 27.2 %collective-permute-start.35 = (bf16[784,384]{1,0:T(8,128)(2,1)S(1)}, bf16[784,384]{1,0:T(8,128)(2,1)S(1)}, u32[]{:S(2)}, u32[]{:S(2)}) collective-permute-start(bf16[784,384]{1,0:T(8,128)(2,1)S(1)} %pad_maximum_fusion.3), channel_id=1, source_target_pairs={{0,4},{2,6},{4,0},{6,2},{8,12},{10,14},{12,8},{14,10},{16,20},{18,... | collective-permute-start | bytes 1806344 | tf_op jit(solution)/shard_map/ppermute | solution.py:405
  394.7 26.6 %collective-permute-start.34 = (bf16[784,384]{1,0:T(8,128)(2,1)S(1)}, bf16[784,384]{1,0:T(8,128)(2,1)S(1)}, u32[]{:S(2)}, u32[]{:S(2)}) collective-permute-start(bf16[784,384]{1,0:T(8,128)(2,1)S(1)} %pad_maximum_fusion.3), channel_id=1, source_target_pairs={{0,6},{2,4},{4,2},{6,0},{8,14},{10,12},{12,10},{14,8},{16,22},{18,... | collective-permute-start | bytes 1806344 | tf_op jit(solution)/shard_map/ppermute | solution.py:405
  (49 other events, 444.4 us)
Sparse Core Ops, SparseCore 0:
  89.4 230.8 all-reduce.3
